TPU v7x, 256 devices: a whole 4x4x8 slice. The times are simulated.
256 devices in a mesh: stream: 16 (over z_hi, y, core), lat: 16 (over z_lo, x).
Axes of the slice: x: 4, y: 4, z: 8 (z_hi: 2, z_lo: 4; z = z_hi * 4 + z_lo), core: 2. Of those that a mesh axis runs over, the one named last changes fastest.
Arguments:
- inverse: bfloat16 [32, 16, 4, 512, 512], P('lat', 'stream'), may hold values from -2 to 2
- upwind: bfloat16 [32, 16, 4, 64, 512], P('lat', 'stream'), may hold values from -0.75 to 0.75
- lateral: bfloat16 [32, 16, 4, 64, 512], P('lat', 'stream'), may hold values from -0.375 to 0.375
- inlet_trace: float32 [32, 64, 256], P('lat'), may hold values from -6 to 6
- previous: bfloat16 [32, 16, 4, 512, 256], P('lat', 'stream'), may hold values from -6 to 6
- uptake_rate: float32 [256], replicated, may hold values from 0.3 to 3
- affinity: float32 [256], replicated, may hold values from 0.5 to 4
- flow_order: int32 [32, 16, 4], P('lat', 'stream'), may hold values from 0 to 3, each once within a row
Outputs:
- concentration: bfloat16 [32, 16, 4, 512, 256], P('lat', 'stream')
Inputs may be any that keep to these rules, and one draw needn't show every extreme that they name: `flow_order`: each row of 4 entries lists 0 to 3 once each.
All inputs are finite; a program needn't handle non-finite values.
Results may differ from a plain program's by a relative error of at most 0.002.
Values sent between devices are 32-bit elements; how exact they have to be, the bound alone decides.
A program may use at most 64 MiB of HBM per device.

v0:
```python
import jax
import jax.numpy as jnp
from jax import lax
from jax.sharding import PartitionSpec as P

NODES_1D = 8
ITERS = 2


HIGHEST = lax.Precision.HIGHEST


def from_behind(value, axis, steps):
    count = lax.axis_size(axis)
    initial, last = (max(0, -steps), min(count, count - steps))
    return lax.ppermute(value, axis, [(source, source + steps) for source in range(initial, last)])


def lateral_face(nodal_field, per_side):
    leading = nodal_field.shape[:-2]
    tracer_count = nodal_field.shape[-1]
    shaped = nodal_field.reshape(leading + (per_side, per_side, per_side, tracer_count))
    return shaped[..., :, per_side - 1, :, :].reshape(leading + (per_side * per_side, tracer_count))


def carry_through(mapping, trace_in):
    return jnp.einsum("cfk,ckg->cfg", mapping, trace_in, precision=HIGHEST)


def per_device(inverse, upwind, lateral, inlet_trace, previous, uptake_rate, affinity, flow_order):
    col_count = inverse.shape[0]
    row_count = inverse.shape[2]
    node_count = inverse.shape[3]
    face_count = upwind.shape[3]
    per_side = NODES_1D
    columns = jnp.arange(col_count)
    order_local = flow_order[:, 0]
    storage_rank = jnp.argsort(order_local, axis=1)
    inverse_local = inverse[:, 0]
    upwind_local = upwind[:, 0]
    lateral_local = lateral[:, 0]
    is_first = lax.axis_index("stream") == 0
    unit_maps = jnp.broadcast_to(
        jnp.eye(face_count, dtype=jnp.float32), (col_count, face_count, face_count)
    )
    current = previous[:, 0].astype(jnp.float32)
    for sweep_index in range(ITERS):
        lagged = current
        traces = lateral_face(lagged, per_side)
        arrived = from_behind(traces[-1:], "lat", 1)
        lateral_in = jnp.concatenate([arrived, traces[:-1]], axis=0)

        def element_step(carried, position):
            inflow, mapping = carried
            chosen = lax.dynamic_index_in_dim(order_local, position, 1, False)
            matrix = inverse_local[columns, chosen].astype(jnp.float32)
            up_part = upwind_local[columns, chosen].astype(jnp.float32)
            side_part = lateral_local[columns, chosen].astype(jnp.float32)
            nodal_lag = lagged[columns, chosen]
            source = uptake_rate * nodal_lag / (1.0 + affinity * jnp.abs(nodal_lag))
            right_side = source + jnp.einsum(
                "cfn,cfg->cng", side_part, lateral_in[columns, chosen], precision=HIGHEST
            )
            right_side = right_side + jnp.einsum("cfn,cfg->cng", up_part, inflow, precision=HIGHEST)
            free_part = jnp.einsum("cmn,cng->cmg", matrix, right_side, precision=HIGHEST)
            lifted = jnp.einsum("cfn,cfk->cnk", up_part, mapping, precision=HIGHEST)
            response = jnp.einsum("cmn,cnk->cmk", matrix, lifted, precision=HIGHEST)
            return (
                (
                    free_part[:, node_count - face_count :, :],
                    response[:, node_count - face_count :, :],
                ),
                (free_part, response),
            )

        initial = (jnp.zeros_like(inlet_trace), unit_maps)
        (offset, transfer_map), (free_all, response_all) = lax.scan(
            element_step, initial, jnp.arange(row_count)
        )

        def relay_turn(turn_index, entering):
            leaving = carry_through(transfer_map, entering) + offset
            passed = from_behind(leaving, "stream", 1)
            return jnp.where(is_first, inlet_trace, passed)

        entering = jnp.where(is_first, inlet_trace, jnp.zeros_like(inlet_trace))
        entering = lax.fori_loop(0, lax.axis_size("stream") - 1, relay_turn, entering)
        solved = free_all + jnp.einsum("rcmk,ckg->rcmg", response_all, entering, precision=HIGHEST)
        placed = jnp.moveaxis(solved, 0, 1)
        current = jnp.take_along_axis(placed, storage_rank[:, :, None, None], axis=1)
    return current[:, None].astype(jnp.bfloat16)


def solution(mesh):
    placed = (
        P("lat", "stream", None, None, None),
        P("lat", "stream", None, None, None),
        P("lat", "stream", None, None, None),
        P("lat", None, None),
        P("lat", "stream", None, None, None),
        P(),
        P(),
        P("lat", "stream", None),
    )
    return jax.shard_map(
        per_device,
        mesh=mesh,
        in_specs=placed,
        out_specs=P("lat", "stream", None, None, None),
        check_vma=False,
    )
```

profile of v0, /device:TPU:160, one launch (start us, length us, event | category | flops | bytes accessed | tf_op | source)
XLA Modules:
  0.0 670.3 jit_solution(7306552116327631919)
XLA Ops:
  21.4 84.5 %while.56 = (s32[]{:T(128)}, f32[2,64,256]{2,1,0:T(8,128)S(1)}, f32[2,64,64]{1,2,0:T(8,128)}, f32[4,2,512,256]{2,3,0,1:T(8,128)}, f32[4,2,512,64]{2,3,0,1:T(8,12...) while((s32[]{:T(128)}, f32[2,64,256]{2,1,0:T(8,128)S(1)}, ...), condition=%wide.region_1.2_spmd.clone, body=%wide.region_0.0_spmd.clone.sunk | while | flops 2468085760 | bytes 19631592 | solution.py:77
  106.8 214.4 %while.54 = (s32[]{:T(128)}, f32[2,64,256]{2,1,0:T(8,128)}, pred[]{:T(512)}, f32[2,64,64]{2,1,0:T(8,128)S(1)}, f32[2,64,256]{2,1,0:T(8,128)S(1)}, /*index=5*/f32[2,64,256]{2,1,0:T(8,128)S(1)}, s32[]{:T(128)}) while((s32[]{:T(128)}, f32[2,64,256]{2,1,0:T(8,128)}, pred[]{:T(512)}, f32[2,64,64]{2,1,0:T(8,128)S(1)}, f32[2,64,256]{2,1,0:T(8,128)S(1)}, ...), condition=%wide.region_3.4_spmd, body=%wide.region_2.3_spmd.sunk | while | flops 25231360 | bytes 1343606 | solution.py:87
  109.9 11.8 %collective-permute-done = f32[2,64,256]{2,1,0:T(8,128)S(1)} collective-permute-done((f32[2,64,256]{2,1,0:T(8,128)S(1)}, f32[2,64,256]{2,1,0:T(8,128)S(1)}, u32[]{:S(2)}, u32[]{:S(2)}) %collective-permute-start) | collective-permute-done | bytes 131104 | tf_op jit(solution)/shard_map/while/body/eval_jaxpr/ppermute | solution.py:16
  125.4 11.4 %collective-permute-done = f32[2,64,256]{2,1,0:T(8,128)S(1)} collective-permute-done((f32[2,64,256]{2,1,0:T(8,128)S(1)}, f32[2,64,256]{2,1,0:T(8,128)S(1)}, u32[]{:S(2)}, u32[]{:S(2)}) %collective-permute-start) | collective-permute-done | bytes 131104 | tf_op jit(solution)/shard_map/while/body/eval_jaxpr/ppermute | solution.py:16
  140.6 10.5 %collective-permute-done = f32[2,64,256]{2,1,0:T(8,128)S(1)} collective-permute-done((f32[2,64,256]{2,1,0:T(8,128)S(1)}, f32[2,64,256]{2,1,0:T(8,128)S(1)}, u32[]{:S(2)}, u32[]{:S(2)}) %collective-permute-start) | collective-permute-done | bytes 131104 | tf_op jit(solution)/shard_map/while/body/eval_jaxpr/ppermute | solution.py:16
  154.8 10.4 %collective-permute-done = f32[2,64,256]{2,1,0:T(8,128)S(1)} collective-permute-done((f32[2,64,256]{2,1,0:T(8,128)S(1)}, f32[2,64,256]{2,1,0:T(8,128)S(1)}, u32[]{:S(2)}, u32[]{:S(2)}) %collective-permute-start) | collective-permute-done | bytes 131104 | tf_op jit(solution)/shard_map/while/body/eval_jaxpr/ppermute | solution.py:16
  168.9 10.4 %collective-permute-done = f32[2,64,256]{2,1,0:T(8,128)S(1)} collective-permute-done((f32[2,64,256]{2,1,0:T(8,128)S(1)}, f32[2,64,256]{2,1,0:T(8,128)S(1)}, u32[]{:S(2)}, u32[]{:S(2)}) %collective-permute-start) | collective-permute-done | bytes 131104 | tf_op jit(solution)/shard_map/while/body/eval_jaxpr/ppermute | solution.py:16
  183.0 10.4 %collective-permute-done = f32[2,64,256]{2,1,0:T(8,128)S(1)} collective-permute-done((f32[2,64,256]{2,1,0:T(8,128)S(1)}, f32[2,64,256]{2,1,0:T(8,128)S(1)}, u32[]{:S(2)}, u32[]{:S(2)}) %collective-permute-start) | collective-permute-done | bytes 131104 | tf_op jit(solution)/shard_map/while/body/eval_jaxpr/ppermute | solution.py:16
  197.2 10.4 %collective-permute-done = f32[2,64,256]{2,1,0:T(8,128)S(1)} collective-permute-done((f32[2,64,256]{2,1,0:T(8,128)S(1)}, f32[2,64,256]{2,1,0:T(8,128)S(1)}, u32[]{:S(2)}, u32[]{:S(2)}) %collective-permute-start) | collective-permute-done | bytes 131104 | tf_op jit(solution)/shard_map/while/body/eval_jaxpr/ppermute | solution.py:16
  211.3 10.4 %collective-permute-done = f32[2,64,256]{2,1,0:T(8,128)S(1)} collective-permute-done((f32[2,64,256]{2,1,0:T(8,128)S(1)}, f32[2,64,256]{2,1,0:T(8,128)S(1)}, u32[]{:S(2)}, u32[]{:S(2)}) %collective-permute-start) | collective-permute-done | bytes 131104 | tf_op jit(solution)/shard_map/while/body/eval_jaxpr/ppermute | solution.py:16
  225.4 10.4 %collective-permute-done = f32[2,64,256]{2,1,0:T(8,128)S(1)} collective-permute-done((f32[2,64,256]{2,1,0:T(8,128)S(1)}, f32[2,64,256]{2,1,0:T(8,128)S(1)}, u32[]{:S(2)}, u32[]{:S(2)}) %collective-permute-start) | collective-permute-done | bytes 131104 | tf_op jit(solution)/shard_map/while/body/eval_jaxpr/ppermute | solution.py:16
  239.5 10.4 %collective-permute-done = f32[2,64,256]{2,1,0:T(8,128)S(1)} collective-permute-done((f32[2,64,256]{2,1,0:T(8,128)S(1)}, f32[2,64,256]{2,1,0:T(8,128)S(1)}, u32[]{:S(2)}, u32[]{:S(2)}) %collective-permute-start) | collective-permute-done | bytes 131104 | tf_op jit(solution)/shard_map/while/body/eval_jaxpr/ppermute | solution.py:16
  253.6 10.4 %collective-permute-done = f32[2,64,256]{2,1,0:T(8,128)S(1)} collective-permute-done((f32[2,64,256]{2,1,0:T(8,128)S(1)}, f32[2,64,256]{2,1,0:T(8,128)S(1)}, u32[]{:S(2)}, u32[]{:S(2)}) %collective-permute-start) | collective-permute-done | bytes 131104 | tf_op jit(solution)/shard_map/while/body/eval_jaxpr/ppermute | solution.py:16
  267.8 10.4 %collective-permute-done = f32[2,64,256]{2,1,0:T(8,128)S(1)} collective-permute-done((f32[2,64,256]{2,1,0:T(8,128)S(1)}, f32[2,64,256]{2,1,0:T(8,128)S(1)}, u32[]{:S(2)}, u32[]{:S(2)}) %collective-permute-start) | collective-permute-done | bytes 131104 | tf_op jit(solution)/shard_map/while/body/eval_jaxpr/ppermute | solution.py:16
  281.9 10.4 %collective-permute-done = f32[2,64,256]{2,1,0:T(8,128)S(1)} collective-permute-done((f32[2,64,256]{2,1,0:T(8,128)S(1)}, f32[2,64,256]{2,1,0:T(8,128)S(1)}, u32[]{:S(2)}, u32[]{:S(2)}) %collective-permute-start) | collective-permute-done | bytes 131104 | tf_op jit(solution)/shard_map/while/body/eval_jaxpr/ppermute | solution.py:16
  296.0 10.4 %collective-permute-done = f32[2,64,256]{2,1,0:T(8,128)S(1)} collective-permute-done((f32[2,64,256]{2,1,0:T(8,128)S(1)}, f32[2,64,256]{2,1,0:T(8,128)S(1)}, u32[]{:S(2)}, u32[]{:S(2)}) %collective-permute-start) | collective-permute-done | bytes 131104 | tf_op jit(solution)/shard_map/while/body/eval_jaxpr/ppermute | solution.py:16
  310.1 10.4 %collective-permute-done = f32[2,64,256]{2,1,0:T(8,128)S(1)} collective-permute-done((f32[2,64,256]{2,1,0:T(8,128)S(1)}, f32[2,64,256]{2,1,0:T(8,128)S(1)}, u32[]{:S(2)}, u32[]{:S(2)}) %collective-permute-start) | collective-permute-done | bytes 131104 | tf_op jit(solution)/shard_map/while/body/eval_jaxpr/ppermute | solution.py:16
  359.6 84.7 %while.57 = (s32[]{:T(128)}, f32[2,64,256]{2,1,0:T(8,128)S(1)}, f32[2,64,64]{1,2,0:T(8,128)}, f32[4,2,512,256]{2,3,0,1:T(8,128)}, f32[4,2,512,64]{2,3,0,1:T(8,12...) while((s32[]{:T(128)}, f32[2,64,256]{2,1,0:T(8,128)S(1)}, ...), condition=%wide.region_6.8_spmd.clone, body=%wide.region_5.7_spmd.clone.sunk | while | flops 2468085760 | bytes 19631592 | solution.py:77
  445.3 212.0 %while.55 = (s32[]{:T(128)}, f32[2,64,256]{2,1,0:T(8,128)}, pred[]{:T(512)}, f32[2,64,64]{2,1,0:T(8,128)S(1)}, f32[2,64,256]{2,1,0:T(8,128)S(1)}, /*index=5*/f32[2,64,256]{2,1,0:T(8,128)S(1)}, s32[]{:T(128)}) while((s32[]{:T(128)}, f32[2,64,256]{2,1,0:T(8,128)}, pred[]{:T(512)}, f32[2,64,64]{2,1,0:T(8,128)S(1)}, f32[2,64,256]{2,1,0:T(8,128)S(1)}, ...), condition=%wide.region_8.10_spmd, body=%wide.region_7.9_spmd.sunk | while | flops 25231360 | bytes 1343606 | solution.py:87
  448.4 10.4 %collective-permute-done.1 = f32[2,64,256]{2,1,0:T(8,128)S(1)} collective-permute-done((f32[2,64,256]{2,1,0:T(8,128)S(1)}, f32[2,64,256]{2,1,0:T(8,128)S(1)}, u32[]{:S(2)}, u32[]{:S(2)}) %collective-permute-start.1) | collective-permute-done | bytes 131104 | tf_op jit(solution)/shard_map/while/body/eval_jaxpr/ppermute | solution.py:16
  462.5 10.4 %collective-permute-done.1 = f32[2,64,256]{2,1,0:T(8,128)S(1)} collective-permute-done((f32[2,64,256]{2,1,0:T(8,128)S(1)}, f32[2,64,256]{2,1,0:T(8,128)S(1)}, u32[]{:S(2)}, u32[]{:S(2)}) %collective-permute-start.1) | collective-permute-done | bytes 131104 | tf_op jit(solution)/shard_map/while/body/eval_jaxpr/ppermute | solution.py:16
  476.7 10.4 %collective-permute-done.1 = f32[2,64,256]{2,1,0:T(8,128)S(1)} collective-permute-done((f32[2,64,256]{2,1,0:T(8,128)S(1)}, f32[2,64,256]{2,1,0:T(8,128)S(1)}, u32[]{:S(2)}, u32[]{:S(2)}) %collective-permute-start.1) | collective-permute-done | bytes 131104 | tf_op jit(solution)/shard_map/while/body/eval_jaxpr/ppermute | solution.py:16
  490.8 10.4 %collective-permute-done.1 = f32[2,64,256]{2,1,0:T(8,128)S(1)} collective-permute-done((f32[2,64,256]{2,1,0:T(8,128)S(1)}, f32[2,64,256]{2,1,0:T(8,128)S(1)}, u32[]{:S(2)}, u32[]{:S(2)}) %collective-permute-start.1) | collective-permute-done | bytes 131104 | tf_op jit(solution)/shard_map/while/body/eval_jaxpr/ppermute | solution.py:16
  504.9 10.4 %collective-permute-done.1 = f32[2,64,256]{2,1,0:T(8,128)S(1)} collective-permute-done((f32[2,64,256]{2,1,0:T(8,128)S(1)}, f32[2,64,256]{2,1,0:T(8,128)S(1)}, u32[]{:S(2)}, u32[]{:S(2)}) %collective-permute-start.1) | collective-permute-done | bytes 131104 | tf_op jit(solution)/shard_map/while/body/eval_jaxpr/ppermute | solution.py:16
  519.1 10.4 %collective-permute-done.1 = f32[2,64,256]{2,1,0:T(8,128)S(1)} collective-permute-done((f32[2,64,256]{2,1,0:T(8,128)S(1)}, f32[2,64,256]{2,1,0:T(8,128)S(1)}, u32[]{:S(2)}, u32[]{:S(2)}) %collective-permute-start.1) | collective-permute-done | bytes 131104 | tf_op jit(solution)/shard_map/while/body/eval_jaxpr/ppermute | solution.py:16
  533.2 10.4 %collective-permute-done.1 = f32[2,64,256]{2,1,0:T(8,128)S(1)} collective-permute-done((f32[2,64,256]{2,1,0:T(8,128)S(1)}, f32[2,64,256]{2,1,0:T(8,128)S(1)}, u32[]{:S(2)}, u32[]{:S(2)}) %collective-permute-start.1) | collective-permute-done | bytes 131104 | tf_op jit(solution)/shard_map/while/body/eval_jaxpr/ppermute | solution.py:16
  547.3 10.4 %collective-permute-done.1 = f32[2,64,256]{2,1,0:T(8,128)S(1)} collective-permute-done((f32[2,64,256]{2,1,0:T(8,128)S(1)}, f32[2,64,256]{2,1,0:T(8,128)S(1)}, u32[]{:S(2)}, u32[]{:S(2)}) %collective-permute-start.1) | collective-permute-done | bytes 131104 | tf_op jit(solution)/shard_map/while/body/eval_jaxpr/ppermute | solution.py:16
  561.5 10.4 %collective-permute-done.1 = f32[2,64,256]{2,1,0:T(8,128)S(1)} collective-permute-done((f32[2,64,256]{2,1,0:T(8,128)S(1)}, f32[2,64,256]{2,1,0:T(8,128)S(1)}, u32[]{:S(2)}, u32[]{:S(2)}) %collective-permute-start.1) | collective-permute-done | bytes 131104 | tf_op jit(solution)/shard_map/while/body/eval_jaxpr/ppermute | solution.py:16
  575.6 10.4 %collective-permute-done.1 = f32[2,64,256]{2,1,0:T(8,128)S(1)} collective-permute-done((f32[2,64,256]{2,1,0:T(8,128)S(1)}, f32[2,64,256]{2,1,0:T(8,128)S(1)}, u32[]{:S(2)}, u32[]{:S(2)}) %collective-permute-start.1) | collective-permute-done | bytes 131104 | tf_op jit(solution)/shard_map/while/body/eval_jaxpr/ppermute | solution.py:16
  589.7 10.4 %collective-permute-done.1 = f32[2,64,256]{2,1,0:T(8,128)S(1)} collective-permute-done((f32[2,64,256]{2,1,0:T(8,128)S(1)}, f32[2,64,256]{2,1,0:T(8,128)S(1)}, u32[]{:S(2)}, u32[]{:S(2)}) %collective-permute-start.1) | collective-permute-done | bytes 131104 | tf_op jit(solution)/shard_map/while/body/eval_jaxpr/ppermute | solution.py:16
  603.9 10.4 %collective-permute-done.1 = f32[2,64,256]{2,1,0:T(8,128)S(1)} collective-permute-done((f32[2,64,256]{2,1,0:T(8,128)S(1)}, f32[2,64,256]{2,1,0:T(8,128)S(1)}, u32[]{:S(2)}, u32[]{:S(2)}) %collective-permute-start.1) | collective-permute-done | bytes 131104 | tf_op jit(solution)/shard_map/while/body/eval_jaxpr/ppermute | solution.py:16
  618.0 10.4 %collective-permute-done.1 = f32[2,64,256]{2,1,0:T(8,128)S(1)} collective-permute-done((f32[2,64,256]{2,1,0:T(8,128)S(1)}, f32[2,64,256]{2,1,0:T(8,128)S(1)}, u32[]{:S(2)}, u32[]{:S(2)}) %collective-permute-start.1) | collective-permute-done | bytes 131104 | tf_op jit(solution)/shard_map/while/body/eval_jaxpr/ppermute | solution.py:16
  (309 shorter events, 360.7 us)
Async XLA Ops:
  4.2 12.0 %collective-permute-start.2 = (f32[1,4,64,256]{3,2,1,0:T(8,128)S(1)}, f32[1,4,64,256]{3,2,1,0:T(8,128)S(1)}, u32[]{:S(2)}, u32[]{:S(2)}) collective-permute-start(f32[1,4,64,256]{3,2,1,0:T(8,128)S(1)} %get-tuple-element.468), channel_id=1, source_target_pairs={{0,1},{1,2},{2,3},{3,4},{4,5},{5,6},{6,7},{7,8},{8,9},{9,10},{10,1... | collective-permute-start | bytes 786440 | tf_op jit(solution)/shard_map/ppermute | solution.py:16
  108.0 13.7 %collective-permute-start = (f32[2,64,256]{2,1,0:T(8,128)S(1)}, f32[2,64,256]{2,1,0:T(8,128)S(1)}, u32[]{:S(2)}, u32[]{:S(2)}) collective-permute-start(f32[2,64,256]{2,1,0:T(8,128)S(1)} %convolution_add_fusion.12), channel_id=1, source_target_pairs={{0,16},{16,32},{32,48},{48,64},{64,80},{80,96},{96,112},{112,128},... | collective-permute-start | bytes 393224 | tf_op jit(solution)/shard_map/while/body/eval_jaxpr/ppermute | solution.py:16
  123.5 13.3 %collective-permute-start = (f32[2,64,256]{2,1,0:T(8,128)S(1)}, f32[2,64,256]{2,1,0:T(8,128)S(1)}, u32[]{:S(2)}, u32[]{:S(2)}) collective-permute-start(f32[2,64,256]{2,1,0:T(8,128)S(1)} %convolution_add_fusion.12), channel_id=1, source_target_pairs={{0,16},{16,32},{32,48},{48,64},{64,80},{80,96},{96,112},{112,128},... | collective-permute-start | bytes 393224 | tf_op jit(solution)/shard_map/while/body/eval_jaxpr/ppermute | solution.py:16
  138.6 12.4 %collective-permute-start = (f32[2,64,256]{2,1,0:T(8,128)S(1)}, f32[2,64,256]{2,1,0:T(8,128)S(1)}, u32[]{:S(2)}, u32[]{:S(2)}) collective-permute-start(f32[2,64,256]{2,1,0:T(8,128)S(1)} %convolution_add_fusion.12), channel_id=1, source_target_pairs={{0,16},{16,32},{32,48},{48,64},{64,80},{80,96},{96,112},{112,128},... | collective-permute-start | bytes 393224 | tf_op jit(solution)/shard_map/while/body/eval_jaxpr/ppermute | solution.py:16
  152.9 12.3 %collective-permute-start = (f32[2,64,256]{2,1,0:T(8,128)S(1)}, f32[2,64,256]{2,1,0:T(8,128)S(1)}, u32[]{:S(2)}, u32[]{:S(2)}) collective-permute-start(f32[2,64,256]{2,1,0:T(8,128)S(1)} %convolution_add_fusion.12), channel_id=1, source_target_pairs={{0,16},{16,32},{32,48},{48,64},{64,80},{80,96},{96,112},{112,128},... | collective-permute-start | bytes 393224 | tf_op jit(solution)/shard_map/while/body/eval_jaxpr/ppermute | solution.py:16
  167.0 12.3 %collective-permute-start = (f32[2,64,256]{2,1,0:T(8,128)S(1)}, f32[2,64,256]{2,1,0:T(8,128)S(1)}, u32[]{:S(2)}, u32[]{:S(2)}) collective-permute-start(f32[2,64,256]{2,1,0:T(8,128)S(1)} %convolution_add_fusion.12), channel_id=1, source_target_pairs={{0,16},{16,32},{32,48},{48,64},{64,80},{80,96},{96,112},{112,128},... | collective-permute-start | bytes 393224 | tf_op jit(solution)/shard_map/while/body/eval_jaxpr/ppermute | solution.py:16
  181.1 12.3 %collective-permute-start = (f32[2,64,256]{2,1,0:T(8,128)S(1)}, f32[2,64,256]{2,1,0:T(8,128)S(1)}, u32[]{:S(2)}, u32[]{:S(2)}) collective-permute-start(f32[2,64,256]{2,1,0:T(8,128)S(1)} %convolution_add_fusion.12), channel_id=1, source_target_pairs={{0,16},{16,32},{32,48},{48,64},{64,80},{80,96},{96,112},{112,128},... | collective-permute-start | bytes 393224 | tf_op jit(solution)/shard_map/while/body/eval_jaxpr/ppermute | solution.py:16
  195.2 12.3 %collective-permute-start = (f32[2,64,256]{2,1,0:T(8,128)S(1)}, f32[2,64,256]{2,1,0:T(8,128)S(1)}, u32[]{:S(2)}, u32[]{:S(2)}) collective-permute-start(f32[2,64,256]{2,1,0:T(8,128)S(1)} %convolution_add_fusion.12), channel_id=1, source_target_pairs={{0,16},{16,32},{32,48},{48,64},{64,80},{80,96},{96,112},{112,128},... | collective-permute-start | bytes 393224 | tf_op jit(solution)/shard_map/while/body/eval_jaxpr/ppermute | solution.py:16
  209.4 12.3 %collective-permute-start = (f32[2,64,256]{2,1,0:T(8,128)S(1)}, f32[2,64,256]{2,1,0:T(8,128)S(1)}, u32[]{:S(2)}, u32[]{:S(2)}) collective-permute-start(f32[2,64,256]{2,1,0:T(8,128)S(1)} %convolution_add_fusion.12), channel_id=1, source_target_pairs={{0,16},{16,32},{32,48},{48,64},{64,80},{80,96},{96,112},{112,128},... | collective-permute-start | bytes 393224 | tf_op jit(solution)/shard_map/while/body/eval_jaxpr/ppermute | solution.py:16
  223.5 12.3 %collective-permute-start = (f32[2,64,256]{2,1,0:T(8,128)S(1)}, f32[2,64,256]{2,1,0:T(8,128)S(1)}, u32[]{:S(2)}, u32[]{:S(2)}) collective-permute-start(f32[2,64,256]{2,1,0:T(8,128)S(1)} %convolution_add_fusion.12), channel_id=1, source_target_pairs={{0,16},{16,32},{32,48},{48,64},{64,80},{80,96},{96,112},{112,128},... | collective-permute-start | bytes 393224 | tf_op jit(solution)/shard_map/while/body/eval_jaxpr/ppermute | solution.py:16
  237.6 12.3 %collective-permute-start = (f32[2,64,256]{2,1,0:T(8,128)S(1)}, f32[2,64,256]{2,1,0:T(8,128)S(1)}, u32[]{:S(2)}, u32[]{:S(2)}) collective-permute-start(f32[2,64,256]{2,1,0:T(8,128)S(1)} %convolution_add_fusion.12), channel_id=1, source_target_pairs={{0,16},{16,32},{32,48},{48,64},{64,80},{80,96},{96,112},{112,128},... | collective-permute-start | bytes 393224 | tf_op jit(solution)/shard_map/while/body/eval_jaxpr/ppermute | solution.py:16
  251.7 12.3 %collective-permute-start = (f32[2,64,256]{2,1,0:T(8,128)S(1)}, f32[2,64,256]{2,1,0:T(8,128)S(1)}, u32[]{:S(2)}, u32[]{:S(2)}) collective-permute-start(f32[2,64,256]{2,1,0:T(8,128)S(1)} %convolution_add_fusion.12), channel_id=1, source_target_pairs={{0,16},{16,32},{32,48},{48,64},{64,80},{80,96},{96,112},{112,128},... | collective-permute-start | bytes 393224 | tf_op jit(solution)/shard_map/while/body/eval_jaxpr/ppermute | solution.py:16
  265.8 12.3 %collective-permute-start = (f32[2,64,256]{2,1,0:T(8,128)S(1)}, f32[2,64,256]{2,1,0:T(8,128)S(1)}, u32[]{:S(2)}, u32[]{:S(2)}) collective-permute-start(f32[2,64,256]{2,1,0:T(8,128)S(1)} %convolution_add_fusion.12), channel_id=1, source_target_pairs={{0,16},{16,32},{32,48},{48,64},{64,80},{80,96},{96,112},{112,128},... | collective-permute-start | bytes 393224 | tf_op jit(solution)/shard_map/while/body/eval_jaxpr/ppermute | solution.py:16
  280.0 12.3 %collective-permute-start = (f32[2,64,256]{2,1,0:T(8,128)S(1)}, f32[2,64,256]{2,1,0:T(8,128)S(1)}, u32[]{:S(2)}, u32[]{:S(2)}) collective-permute-start(f32[2,64,256]{2,1,0:T(8,128)S(1)} %convolution_add_fusion.12), channel_id=1, source_target_pairs={{0,16},{16,32},{32,48},{48,64},{64,80},{80,96},{96,112},{112,128},... | collective-permute-start | bytes 393224 | tf_op jit(solution)/shard_map/while/body/eval_jaxpr/ppermute | solution.py:16
  294.1 12.3 %collective-permute-start = (f32[2,64,256]{2,1,0:T(8,128)S(1)}, f32[2,64,256]{2,1,0:T(8,128)S(1)}, u32[]{:S(2)}, u32[]{:S(2)}) collective-permute-start(f32[2,64,256]{2,1,0:T(8,128)S(1)} %convolution_add_fusion.12), channel_id=1, source_target_pairs={{0,16},{16,32},{32,48},{48,64},{64,80},{80,96},{96,112},{112,128},... | collective-permute-start | bytes 393224 | tf_op jit(solution)/shard_map/while/body/eval_jaxpr/ppermute | solution.py:16
  308.2 12.3 %collective-permute-start = (f32[2,64,256]{2,1,0:T(8,128)S(1)}, f32[2,64,256]{2,1,0:T(8,128)S(1)}, u32[]{:S(2)}, u32[]{:S(2)}) collective-permute-start(f32[2,64,256]{2,1,0:T(8,128)S(1)} %convolution_add_fusion.12), channel_id=1, source_target_pairs={{0,16},{16,32},{32,48},{48,64},{64,80},{80,96},{96,112},{112,128},... | collective-permute-start | bytes 393224 | tf_op jit(solution)/shard_map/while/body/eval_jaxpr/ppermute | solution.py:16
  344.1 10.4 %collective-permute-start.3 = (f32[1,4,64,256]{3,2,1,0:T(8,128)S(1)}, f32[1,4,64,256]{3,2,1,0:T(8,128)S(1)}, u32[]{:S(2)}, u32[]{:S(2)}) collective-permute-start(f32[1,4,64,256]{3,2,1,0:T(8,128)S(1)} %get-tuple-element.466), channel_id=1, source_target_pairs={{0,1},{1,2},{2,3},{3,4},{4,5},{5,6},{6,7},{7,8},{8,9},{9,10},{10,1... | collective-permute-start | bytes 786440 | tf_op jit(solution)/shard_map/ppermute | solution.py:16
  446.5 12.3 %collective-permute-start.1 = (f32[2,64,256]{2,1,0:T(8,128)S(1)}, f32[2,64,256]{2,1,0:T(8,128)S(1)}, u32[]{:S(2)}, u32[]{:S(2)}) collective-permute-start(f32[2,64,256]{2,1,0:T(8,128)S(1)} %convolution_add_fusion.13), channel_id=1, source_target_pairs={{0,16},{16,32},{32,48},{48,64},{64,80},{80,96},{96,112},{112,128},... | collective-permute-start | bytes 393224 | tf_op jit(solution)/shard_map/while/body/eval_jaxpr/ppermute | solution.py:16
  460.6 12.3 %collective-permute-start.1 = (f32[2,64,256]{2,1,0:T(8,128)S(1)}, f32[2,64,256]{2,1,0:T(8,128)S(1)}, u32[]{:S(2)}, u32[]{:S(2)}) collective-permute-start(f32[2,64,256]{2,1,0:T(8,128)S(1)} %convolution_add_fusion.13), channel_id=1, source_target_pairs={{0,16},{16,32},{32,48},{48,64},{64,80},{80,96},{96,112},{112,128},... | collective-permute-start | bytes 393224 | tf_op jit(solution)/shard_map/while/body/eval_jaxpr/ppermute | solution.py:16
  474.7 12.3 %collective-permute-start.1 = (f32[2,64,256]{2,1,0:T(8,128)S(1)}, f32[2,64,256]{2,1,0:T(8,128)S(1)}, u32[]{:S(2)}, u32[]{:S(2)}) collective-permute-start(f32[2,64,256]{2,1,0:T(8,128)S(1)} %convolution_add_fusion.13), channel_id=1, source_target_pairs={{0,16},{16,32},{32,48},{48,64},{64,80},{80,96},{96,112},{112,128},... | collective-permute-start | bytes 393224 | tf_op jit(solution)/shard_map/while/body/eval_jaxpr/ppermute | solution.py:16
  488.9 12.3 %collective-permute-start.1 = (f32[2,64,256]{2,1,0:T(8,128)S(1)}, f32[2,64,256]{2,1,0:T(8,128)S(1)}, u32[]{:S(2)}, u32[]{:S(2)}) collective-permute-start(f32[2,64,256]{2,1,0:T(8,128)S(1)} %convolution_add_fusion.13), channel_id=1, source_target_pairs={{0,16},{16,32},{32,48},{48,64},{64,80},{80,96},{96,112},{112,128},... | collective-permute-start | bytes 393224 | tf_op jit(solution)/shard_map/while/body/eval_jaxpr/ppermute | solution.py:16
  503.0 12.3 %collective-permute-start.1 = (f32[2,64,256]{2,1,0:T(8,128)S(1)}, f32[2,64,256]{2,1,0:T(8,128)S(1)}, u32[]{:S(2)}, u32[]{:S(2)}) collective-permute-start(f32[2,64,256]{2,1,0:T(8,128)S(1)} %convolution_add_fusion.13), channel_id=1, source_target_pairs={{0,16},{16,32},{32,48},{48,64},{64,80},{80,96},{96,112},{112,128},... | collective-permute-start | bytes 393224 | tf_op jit(solution)/shard_map/while/body/eval_jaxpr/ppermute | solution.py:16
  517.1 12.3 %collective-permute-start.1 = (f32[2,64,256]{2,1,0:T(8,128)S(1)}, f32[2,64,256]{2,1,0:T(8,128)S(1)}, u32[]{:S(2)}, u32[]{:S(2)}) collective-permute-start(f32[2,64,256]{2,1,0:T(8,128)S(1)} %convolution_add_fusion.13), channel_id=1, source_target_pairs={{0,16},{16,32},{32,48},{48,64},{64,80},{80,96},{96,112},{112,128},... | collective-permute-start | bytes 393224 | tf_op jit(solution)/shard_map/while/body/eval_jaxpr/ppermute | solution.py:16
  531.3 12.3 %collective-permute-start.1 = (f32[2,64,256]{2,1,0:T(8,128)S(1)}, f32[2,64,256]{2,1,0:T(8,128)S(1)}, u32[]{:S(2)}, u32[]{:S(2)}) collective-permute-start(f32[2,64,256]{2,1,0:T(8,128)S(1)} %convolution_add_fusion.13), channel_id=1, source_target_pairs={{0,16},{16,32},{32,48},{48,64},{64,80},{80,96},{96,112},{112,128},... | collective-permute-start | bytes 393224 | tf_op jit(solution)/shard_map/while/body/eval_jaxpr/ppermute | solution.py:16
  545.4 12.3 %collective-permute-start.1 = (f32[2,64,256]{2,1,0:T(8,128)S(1)}, f32[2,64,256]{2,1,0:T(8,128)S(1)}, u32[]{:S(2)}, u32[]{:S(2)}) collective-permute-start(f32[2,64,256]{2,1,0:T(8,128)S(1)} %convolution_add_fusion.13), channel_id=1, source_target_pairs={{0,16},{16,32},{32,48},{48,64},{64,80},{80,96},{96,112},{112,128},... | collective-permute-start | bytes 393224 | tf_op jit(solution)/shard_map/while/body/eval_jaxpr/ppermute | solution.py:16
  559.5 12.3 %collective-permute-start.1 = (f32[2,64,256]{2,1,0:T(8,128)S(1)}, f32[2,64,256]{2,1,0:T(8,128)S(1)}, u32[]{:S(2)}, u32[]{:S(2)}) collective-permute-start(f32[2,64,256]{2,1,0:T(8,128)S(1)} %convolution_add_fusion.13), channel_id=1, source_target_pairs={{0,16},{16,32},{32,48},{48,64},{64,80},{80,96},{96,112},{112,128},... | collective-permute-start | bytes 393224 | tf_op jit(solution)/shard_map/while/body/eval_jaxpr/ppermute | solution.py:16
  573.7 12.3 %collective-permute-start.1 = (f32[2,64,256]{2,1,0:T(8,128)S(1)}, f32[2,64,256]{2,1,0:T(8,128)S(1)}, u32[]{:S(2)}, u32[]{:S(2)}) collective-permute-start(f32[2,64,256]{2,1,0:T(8,128)S(1)} %convolution_add_fusion.13), channel_id=1, source_target_pairs={{0,16},{16,32},{32,48},{48,64},{64,80},{80,96},{96,112},{112,128},... | collective-permute-start | bytes 393224 | tf_op jit(solution)/shard_map/while/body/eval_jaxpr/ppermute | solution.py:16
  587.8 12.3 %collective-permute-start.1 = (f32[2,64,256]{2,1,0:T(8,128)S(1)}, f32[2,64,256]{2,1,0:T(8,128)S(1)}, u32[]{:S(2)}, u32[]{:S(2)}) collective-permute-start(f32[2,64,256]{2,1,0:T(8,128)S(1)} %convolution_add_fusion.13), channel_id=1, source_target_pairs={{0,16},{16,32},{32,48},{48,64},{64,80},{80,96},{96,112},{112,128},... | collective-permute-start | bytes 393224 | tf_op jit(solution)/shard_map/while/body/eval_jaxpr/ppermute | solution.py:16
  601.9 12.3 %collective-permute-start.1 = (f32[2,64,256]{2,1,0:T(8,128)S(1)}, f32[2,64,256]{2,1,0:T(8,128)S(1)}, u32[]{:S(2)}, u32[]{:S(2)}) collective-permute-start(f32[2,64,256]{2,1,0:T(8,128)S(1)} %convolution_add_fusion.13), channel_id=1, source_target_pairs={{0,16},{16,32},{32,48},{48,64},{64,80},{80,96},{96,112},{112,128},... | collective-permute-start | bytes 393224 | tf_op jit(solution)/shard_map/while/body/eval_jaxpr/ppermute | solution.py:16
  616.1 12.3 %collective-permute-start.1 = (f32[2,64,256]{2,1,0:T(8,128)S(1)}, f32[2,64,256]{2,1,0:T(8,128)S(1)}, u32[]{:S(2)}, u32[]{:S(2)}) collective-permute-start(f32[2,64,256]{2,1,0:T(8,128)S(1)} %convolution_add_fusion.13), channel_id=1, source_target_pairs={{0,16},{16,32},{32,48},{48,64},{64,80},{80,96},{96,112},{112,128},... | collective-permute-start | bytes 393224 | tf_op jit(solution)/shard_map/while/body/eval_jaxpr/ppermute | solution.py:16
  630.2 12.3 %collective-permute-start.1 = (f32[2,64,256]{2,1,0:T(8,128)S(1)}, f32[2,64,256]{2,1,0:T(8,128)S(1)}, u32[]{:S(2)}, u32[]{:S(2)}) collective-permute-start(f32[2,64,256]{2,1,0:T(8,128)S(1)} %convolution_add_fusion.13), channel_id=1, source_target_pairs={{0,16},{16,32},{32,48},{48,64},{64,80},{80,96},{96,112},{112,128},... | collective-permute-start | bytes 393224 | tf_op jit(solution)/shard_map/while/body/eval_jaxpr/ppermute | solution.py:16
  644.3 12.3 %collective-permute-start.1 = (f32[2,64,256]{2,1,0:T(8,128)S(1)}, f32[2,64,256]{2,1,0:T(8,128)S(1)}, u32[]{:S(2)}, u32[]{:S(2)}) collective-permute-start(f32[2,64,256]{2,1,0:T(8,128)S(1)} %convolution_add_fusion.13), channel_id=1, source_target_pairs={{0,16},{16,32},{32,48},{48,64},{64,80},{80,96},{96,112},{112,128},... | collective-permute-start | bytes 393224 | tf_op jit(solution)/shard_map/while/body/eval_jaxpr/ppermute | solution.py:16
  (24 other events, 129.8 us)
where the time goes:
time: 675 us; the launch traced here: 670 us
  waiting for transfers between devices  329 us (49%)
  local copies, waits for them, and re-layouts  134 us (20%)
  matrix products  92.5 us (14%)
  starting transfers between devices  63.1 us (9%)
  other arithmetic  35.5 us (5%)
  loops' own time  16.4 us (2%)
    ppermute x32, waiting for transfers between devices, from_behind(): lax.ppermute(value, axis, [(source, source + steps) for source in range(i...  329 us
    ppermute x32, starting transfers between devices, from_behind(): lax.ppermute(value, axis, [(source, source + steps) for source in range(i...  63.1 us
    dot_general x30, matrix products, carry_through(): return jnp.einsum('cfk,ckg->cfg', mapping, trace_in, precision=HIGHEST)  34.6 us
    gather x8, local copies, waits for them, and re-layouts, element_step(): matrix = inverse_local[columns, chosen].astype(jnp.float32)  22.4 us
    gather x8, local copies, waits for them, and re-layouts, element_step(): nodal_lag = lagged[columns, chosen]  22.4 us
    select_n x30, other arithmetic, relay_turn(): return jnp.where(is_first, inlet_trace, passed)  19.9 us
    another operation x2, loops' own time, per_device(): lax.scan(element_step, initial, jnp.arange(row_count))  15.9 us
    gather x5, local copies, waits for them, and re-layouts, per_device(): jnp.take_along_axis(placed, storage_rank[:, :, None, None], axis=1)  15.1 us
  transfers between devices with their start and end apart: 32, of which 32 were waited for; matrix products, arithmetic and copies ran while one was open for 0% of the time, Pallas kernels for 0%

commit v1 on v0

v1 whole, which is shorter than its diff:
```python
import functools

import jax
import jax.numpy as jnp
from jax import lax
from jax.experimental import pallas as pl
from jax.experimental.pallas import tpu as pltpu
from jax.sharding import PartitionSpec as P

MESH = pl.DeviceIdType.MESH
F32 = jnp.float32
BF16 = jnp.bfloat16
YS = 4


def split(x):
    hi = x.astype(BF16)
    return hi, (x - hi.astype(F32)).astype(BF16)


def dot(a, b):
    return jnp.dot(a, b, preferred_element_type=F32)


def dot_nt(a, b):
    return lax.dot_general(a, b, (((1,), (1,)), ((), ())), preferred_element_type=F32)


def dot3(ah, al, b):
    bh, bl = split(b)
    return dot(ah, bh) + (dot(al, bh) + dot(ah, bl))


def cat0(*xs):
    return jnp.concatenate(xs, axis=0)


def kernel(
    order, inv, up, side, inlet, prev, upt, aff, out,
    A, UL, PV, MN, F, SRC, LS, LR, LAT, H, G, INF, TT, TP, TC, THL, VV,
    OS, OR, OC, X8S, X8R, YSND, XIN,
    ld_sem, lat_s, lat_r, t_s, t_r, tc_s, tc_r, s1_s, s1_r, s2_s, s2_r, z_s, z_r, s4_s, s4_r,
):
    cols, rows, nodes, face = 2, 4, 512, 64
    half = 128
    edge = nodes - face
    s = lax.axis_index("stream")
    lat = lax.axis_index("lat")
    lats = lax.axis_size("lat")
    core = lax.rem(s, 2)
    y = lax.rem(s // 2, YS)
    zhi = s // (2 * YS)
    is0 = core == 0
    partner = {"stream": s + 1 - 2 * core}

    def ypeer(d):
        return {"stream": zhi * (2 * YS) + lax.rem(y + d, YS) * 2 + core}

    zpeer = {"stream": lax.rem(s + 2 * YS, 4 * YS)}

    loads = {}

    def load(name, k, src, dst):
        c = pltpu.make_async_copy(src, dst, ld_sem.at[k])
        c.start()
        loads[name] = c

    load("prev1", 0, prev.at[1, 0], PV.at[1])
    load("u0", 2, up.at[0, 0], UL.at[0, :, 0:face])
    load("l0", 4, side.at[0, 0], UL.at[0, :, face:])
    load("al0", 6, inv.at[0, 0, :, edge:], A.at[0, :, edge:])
    load("u1", 3, up.at[1, 0], UL.at[1, :, 0:face])
    load("l1", 5, side.at[1, 0], UL.at[1, :, face:])
    load("al1", 7, inv.at[1, 0, :, edge:], A.at[1, :, edge:])
    load("prev0", 1, prev.at[0, 0], PV.at[0])
    load("ar1", 9, inv.at[1, 0, :, 0:edge], A.at[1, :, 0:edge])
    load("ar0", 8, inv.at[0, 0, :, 0:edge], A.at[0, :, 0:edge])

    barrier = pltpu.get_barrier_semaphore()
    peers = [partner, ypeer(1), ypeer(2), ypeer(3), zpeer]
    peers += [{"lat": lax.rem(lat + 1, lats)}, {"lat": lax.rem(lat + lats - 1, lats)}]
    for peer in peers:
        pl.semaphore_signal(barrier, inc=1, device_id=peer, device_id_type=MESH)

    def remote(src, dst, ssem, rsem, peer):
        return pltpu.make_async_remote_copy(
            src_ref=src, dst_ref=dst, send_sem=ssem, recv_sem=rsem, device_id=peer, device_id_type=MESH
        )

    def lat_copy(it):
        return remote(LS.at[it], LR.at[it], lat_s.at[it], lat_r.at[it], {"lat": lax.rem(lat + 1, lats)})

    def lat_send(it):
        @pl.when(lat < lats - 1)
        def _():
            lat_copy(it).start()

    def prev_trace(c, j):
        parts = []
        for a in range(8):
            piece = PV[c, j, a * 64 + 48 : a * 64 + 64, :].astype(F32)
            parts.append(piece[8:16])
        return cat0(*parts)

    def value_trace(x):
        return cat0(*[x[a * 64 + 56 : a * 64 + 64] for a in range(8)])

    loads["prev1"].wait()
    for j in range(rows):
        LS[0, j] = prev_trace(1, j)
    pl.semaphore_wait(barrier, len(peers))
    lat_send(0)

    for c in range(cols):
        for n in ("u", "l", "al"):
            loads[n + str(c)].wait()
        for j in range(rows):
            hi, lo = split(dot_nt(A[c, j, edge:, :], UL[c, j]))
            MN[c, j, edge:, 0:128] = hi
            MN[c, j, edge:, 128:256] = lo

    def mn_edge(c, j):
        return MN[c, j, edge:, :]

    def apply(mn4, rh, rl):
        return dot(mn4, cat0(rh, rh)) + dot(mn4[:, 0:128], rl)

    zero64 = jnp.zeros((face, face), BF16)
    for c in range(cols):
        first = mn_edge(c, order[c, 0, 0])
        g = first[:, 0:face].astype(F32) + first[:, 128 : 128 + face].astype(F32)
        for p in range(1, rows + 1):
            gh, gl = split(g)
            if p < rows:
                G[c, 0, (p - 1) * face : p * face, :] = gh
                G[c, 1, (p - 1) * face : p * face, :] = gl
                g = apply(mn_edge(c, order[c, 0, p]), cat0(gh, zero64), cat0(gl, zero64))
        TT[c] = g
    t_copy = remote(TT, TP, t_s, t_r, partner)
    t_copy.start()

    loads["prev0"].wait()
    for j in range(rows):
        LAT[0, 1, j] = prev_trace(0, j).astype(BF16)
        LAT[1, 1, j] = jnp.zeros((face, 256), BF16)
    for c in range(cols):
        piece = jnp.where(is0, inlet[c, :, 0:half], inlet[c, :, half:])
        piece = jnp.where(zhi == 0, piece, jnp.zeros_like(piece))
        for it in range(2):
            OC[it, c, YS] = piece

    rate = upt[...].reshape(1, 256)
    affinity = aff[...].reshape(1, 256)

    def source_of(x):
        return rate * x / (1.0 + affinity * jnp.abs(x))

    def put_source(c, j, x):
        hi, lo = split(source_of(x))
        SRC[c, 0, j] = hi
        SRC[c, 1, j] = lo
        a = A[c, j, edge:, :]
        F[c, j, edge:, :] = dot(a, hi) + dot(a, lo)

    def first_source(c):
        def body(j, _):
            put_source(c, j, PV[c, j].astype(F32))
            return 0

        lax.fori_loop(0, rows, body, 0)

    def rest(c):
        def body(j, _):
            a = A[c, j, 0:edge, :]
            F[c, j, 0:edge, :] = dot(a, SRC[c, 0, j]) + dot(a, SRC[c, 1, j])
            return 0

        lax.fori_loop(0, rows, body, 0)

    def maps_rest(c):
        def body(j, _):
            hi, lo = split(dot_nt(A[c, j, 0:edge, :], UL[c, j]))
            MN[c, j, 0:edge, 0:128] = hi
            MN[c, j, 0:edge, 128:256] = lo
            return 0

        lax.fori_loop(0, rows, body, 0)

    zero_trace = jnp.zeros((face, 256), BF16)

    def s1_copy(it, c):
        return remote(OS.at[it, c, 1 - core], OR.at[it, c], s1_s.at[it, c], s1_r.at[it, c], partner)

    def chain(it, c):
        drive = []
        for p in range(rows):
            j = order[c, 0, p]
            lh, ll = LAT[0, c, j], LAT[1, c, j]
            drive.append(F[c, j, edge:, :] + apply(mn_edge(c, j), cat0(zero_trace, lh), cat0(zero_trace, ll)))
        h = drive[0]
        for p in range(1, rows):
            H[c, p - 1] = h
            hh, hl = split(h)
            h = drive[p] + apply(mn_edge(c, order[c, 0, p]), cat0(hh, zero_trace), cat0(hl, zero_trace))
        OS[it, c, 0] = h[:, 0:half]
        OS[it, c, 1] = h[:, half:]
        s1_copy(it, c).start()

    def first_second(it, c):
        own, got = OS[it, c, core], OR[it, c]
        return jnp.where(is0, own, got), jnp.where(is0, got, own)

    def s2_copy(it, c, d):
        return remote(OC.at[it, c, y], OC.at[it, c, y], s2_s.at[it, c, d - 1], s2_r.at[it, c, y], ypeer(d))

    def s2_arrival(it, c, d):
        source = lax.rem(y + d, YS)
        return remote(OC.at[it, c, source], OC.at[it, c, source], s2_s.at[it, c, d - 1], s2_r.at[it, c, source], ypeer(d))

    def compose(it, c):
        s1_copy(it, c).wait_recv()
        o_first, o_second = first_second(it, c)
        OC[it, c, y] = dot3(THL[1, c, 0], THL[1, c, 1], o_first) + o_second
        for d in (2, 1, 3):
            s2_copy(it, c, d).start()

    def z_copy(it, c):
        return remote(X8S.at[it, c], X8R.at[it, c], z_s.at[it, c], z_r.at[it, c], zpeer)

    def s4_copy(it, c):
        return remote(YSND.at[it, c], XIN.at[it, c, core], s4_s.at[it, c], s4_r.at[it, c], partner)

    def s4_arrival(it, c):
        return remote(YSND.at[it, c], XIN.at[it, c, 1 - core], s4_s.at[it, c], s4_r.at[it, c], partner)

    def put_entering(it, c, q):
        YSND[it, c] = jnp.where(is0, q[face:], q[0:face])
        XIN[it, c, core] = jnp.where(is0, q[0:face], q[face:])

    def gather(it, c):
        for d in (1, 3, 2):
            s2_arrival(it, c, d).wait_recv()
        offsets = OC[it, c].reshape((YS + 1) * face, half)
        q = dot3(VV[c, 0], VV[c, 1], offsets)
        o_first, _ = first_second(it, c)
        q = cat0(q[0:face], q[face : 2 * face] + o_first, q[2 * face :])

        @pl.when(zhi == 0)
        def _():
            X8S[it, c] = q[2 * face :]
            z_copy(it, c).start()
            put_entering(it, c, q[0 : 2 * face])
            s4_copy(it, c).start()

        @pl.when(zhi == 1)
        def _():
            X8S[it, c] = q[0:face]
            YSND[it, c] = q[face : 2 * face]

    def carry(it, c):
        @pl.when(zhi == 1)
        def _():
            z_copy(it, c).wait_recv()
            q = cat0(X8S[it, c], YSND[it, c])
            v = slice(YS * face, (YS + 1) * face)
            q = q + dot3(VV[c, 0, 0 : 2 * face, v], VV[c, 1, 0 : 2 * face, v], X8R[it, c])
            put_entering(it, c, q)
            s4_copy(it, c).start()

    def inflows(it, c):
        s4_arrival(it, c).wait_recv()
        x = jnp.concatenate([XIN[it, c, 0], XIN[it, c, 1]], axis=1)
        xh, xl = split(x)
        INF[0, c, 0] = xh
        INF[1, c, 0] = xl
        later = dot(G[c, 0], xh) + (dot(G[c, 1], xh) + dot(G[c, 0], xl))
        for p in range(1, rows):
            xh, xl = split(later[(p - 1) * face : p * face] + H[c, p - 1])
            INF[0, c, p] = xh
            INF[1, c, p] = xl

    def rank_of(c, j):
        rank = jnp.int32(0)
        for p in range(1, rows):
            rank = jnp.where(order[c, 0, p] == j, p, rank)
        return rank

    def solved(c, j):
        rank = rank_of(c, j)
        rh = cat0(INF[0, c, rank], LAT[0, c, j])
        rl = cat0(INF[1, c, rank], LAT[1, c, j])
        return F[c, j] + apply(MN[c, j], rh, rl)

    def lag(c):
        def body(j, _):
            x = solved(c, j)
            trace = value_trace(x)
            if c == 1:
                LS[1, j] = trace
            else:
                hi, lo = split(trace)
                LAT[0, 1, j] = hi
                LAT[1, 1, j] = lo
            put_source(c, j, x)
            return 0

        lax.fori_loop(0, rows, body, 0)

    def finish(c):
        def body(j, _):
            out[c, 0, j] = solved(c, j).astype(BF16)
            return 0

        lax.fori_loop(0, rows, body, 0)

    def lat_arrival(it):
        @pl.when(lat > 0)
        def _():
            lat_copy(it).wait_recv()
            for j in range(rows):
                hi, lo = split(LR[it, j])
                LAT[0, 0, j] = hi
                LAT[1, 0, j] = lo

        @pl.when(lat == 0)
        def _():
            for j in range(rows):
                LAT[0, 0, j] = zero_trace
                LAT[1, 0, j] = zero_trace

    first_source(1)

    t_copy.wait_recv()
    for c in range(cols):
        own, got = TT[c], TP[c]
        t0h, t0l = split(jnp.where(is0, own, got))
        t1h, t1l = split(jnp.where(is0, got, own))
        THL[0, c, 0], THL[0, c, 1], THL[1, c, 0], THL[1, c, 1] = t0h, t0l, t1h, t1l
        TC[y, c] = dot3(t1h, t1l, jnp.where(is0, own, got))

    def tc_copy(d):
        return remote(TC.at[y], TC.at[y], tc_s.at[d - 1], tc_r.at[y], ypeer(d))

    def tc_arrival(d):
        source = lax.rem(y + d, YS)
        return remote(TC.at[source], TC.at[source], tc_s.at[d - 1], tc_r.at[source], ypeer(d))

    for d in (2, 1, 3):
        tc_copy(d).start()

    chain(0, 1)
    first_source(0)
    compose(0, 1)

    for d in (1, 3, 2):
        tc_arrival(d).wait_recv()
    width = (YS + 1) * face
    row_id = lax.broadcasted_iota(jnp.int32, (face, width), 0)
    lane_id = lax.broadcasted_iota(jnp.int32, (face, width), 1)

    def unit(block):
        return jnp.where(lane_id - face * block == row_id, 1.0, 0.0).astype(F32)

    for c in range(cols):
        x = unit(YS)
        mine = jnp.where(y == 0, x, jnp.zeros_like(x))
        for t in range(YS):
            if t == 0:
                x = cat_lanes(TC[0, c], width) + unit(0)
            else:
                th, tl = split(TC[t, c])
                x = dot3(th, tl, x) + unit(t)
            if t + 1 < YS:
                mine = jnp.where(y == t + 1, x, mine)
        both = dot3(THL[0, c, 0], THL[0, c, 1], mine)
        vh, vl = split(cat0(mine, both, x))
        VV[c, 0] = vh
        VV[c, 1] = vl

    lat_arrival(0)
    chain(0, 0)
    loads["ar1"].wait()
    maps_rest(1)
    compose(0, 0)
    rest(1)
    gather(0, 1)
    loads["ar0"].wait()
    maps_rest(0)
    rest(0)
    gather(0, 0)
    carry(0, 1)
    inflows(0, 1)
    lag(1)
    lat_send(1)
    carry(0, 0)
    inflows(0, 0)
    lag(0)

    chain(1, 1)
    rest(1)
    compose(1, 1)
    lat_arrival(1)
    chain(1, 0)
    rest(0)
    compose(1, 0)
    gather(1, 1)
    carry(1, 1)
    gather(1, 0)
    carry(1, 0)
    inflows(1, 1)
    finish(1)
    inflows(1, 0)
    finish(0)

    t_copy.wait_send()
    for d in range(1, YS):
        tc_copy(d).wait_send()
    for it in range(2):
        for c in range(cols):
            s1_copy(it, c).wait_send()
            s4_copy(it, c).wait_send()
            for d in range(1, YS):
                s2_copy(it, c, d).wait_send()

            @pl.when(zhi == 0)
            def _():
                z_copy(it, c).wait_send()

        @pl.when(lat < lats - 1)
        def _():
            lat_copy(it).wait_send()


def cat_lanes(t, width):
    face = t.shape[0]
    return jnp.concatenate([jnp.zeros((face, width - face), F32), t], axis=1)


def per_device(inverse, upwind, lateral, inlet_trace, previous, uptake_rate, affinity, flow_order):
    any_space = pl.BlockSpec(memory_space=pltpu.HBM)
    vmem = pl.BlockSpec(memory_space=pltpu.VMEM)
    dma = pltpu.SemaphoreType.DMA
    scratch = [
        pltpu.VMEM((2, 4, 512, 512), BF16),
        pltpu.VMEM((2, 4, 128, 512), BF16),
        pltpu.VMEM((2, 4, 512, 256), BF16),
        pltpu.VMEM((2, 4, 512, 256), BF16),
        pltpu.VMEM((2, 4, 512, 256), F32),
        pltpu.VMEM((2, 2, 4, 512, 256), BF16),
        pltpu.VMEM((2, 4, 64, 256), F32),
        pltpu.VMEM((2, 4, 64, 256), F32),
        pltpu.VMEM((2, 2, 4, 64, 256), BF16),
        pltpu.VMEM((2, 3, 64, 256), F32),
        pltpu.VMEM((2, 2, 192, 64), BF16),
        pltpu.VMEM((2, 2, 4, 64, 256), BF16),
        pltpu.VMEM((2, 64, 64), F32),
        pltpu.VMEM((2, 64, 64), F32),
        pltpu.VMEM((4, 2, 64, 64), F32),
        pltpu.VMEM((2, 2, 2, 64, 64), BF16),
        pltpu.VMEM((2, 2, 192, 320), BF16),
        pltpu.VMEM((2, 2, 2, 64, 128), F32),
        pltpu.VMEM((2, 2, 64, 128), F32),
        pltpu.VMEM((2, 2, 5, 64, 128), F32),
        pltpu.VMEM((2, 2, 64, 128), F32),
        pltpu.VMEM((2, 2, 64, 128), F32),
        pltpu.VMEM((2, 2, 64, 128), F32),
        pltpu.VMEM((2, 2, 2, 64, 128), F32),
        dma((10,)),
        dma((2,)), dma((2,)),
        dma, dma,
        dma((3,)), dma((4,)),
        dma((2, 2)), dma((2, 2)),
        dma((2, 2, 3)), dma((2, 2, 4)),
        dma((2, 2)), dma((2, 2)),
        dma((2, 2)), dma((2, 2)),
    ]
    return pl.pallas_call(
        kernel,
        out_shape=jax.ShapeDtypeStruct(previous.shape, BF16),
        in_specs=[
            pl.BlockSpec(memory_space=pltpu.SMEM),
            any_space, any_space, any_space, vmem, any_space, vmem, vmem,
        ],
        out_specs=vmem,
        scratch_shapes=scratch,
        compiler_params=pltpu.CompilerParams(
            collective_id=0, has_side_effects=True, vmem_limit_bytes=60 * 1024 * 1024
        ),
    )(flow_order, inverse, upwind, lateral, inlet_trace, previous, uptake_rate, affinity)


def solution(mesh):
    placed = (
        P("lat", "stream", None, None, None),
        P("lat", "stream", None, None, None),
        P("lat", "stream", None, None, None),
        P("lat", None, None),
        P("lat", "stream", None, None, None),
        P(),
        P(),
        P("lat", "stream", None),
    )
    return jax.shard_map(
        per_device,
        mesh=mesh,
        in_specs=placed,
        out_specs=P("lat", "stream", None, None, None),
        check_vma=False,
    )
```

time: 675 us -> 53.7 us (0.08)
  the two profiles are of different devices: /device:TPU:160 before, /device:TPU:225 now
where the time goes in v1:
time: 53.7 us; the launch traced here: 53.5 us
  Pallas kernels  50.4 us (94%)
  local copies, waits for them, and re-layouts  3.05 us (6%)
    pallas_call x1, Pallas kernels, per_device(): pl.pallas_call(kernel, out_shape=jax.ShapeDtypeStruct(previous.shape, BF1...  50.4 us
    unnamed x1, local copies, waits for them, and re-layouts  3.05 us

profile of v1, /device:TPU:225, one launch (start us, length us, event | category | flops | bytes accessed | tf_op | source)
XLA Modules:
  0.0 53.5 jit_solution(1096313487355880354)
XLA Ops:
  0.0 50.4 %shard_map.82 = bf16[2,1,4,512,256]{4,3,2,1,0:T(8,128)(2,1)} custom-call(s32[2,1,4]{2,1,0:T(1,128)} %order.1, bf16[2,1,4,512,512]{4,3,2,1,0:T(8,128)(2,1)} %inv.1, bf16[2,1,4,64,512]{4,3,2,1,0:T(8,128)(2,1)} %up.1, bf16[2,1,4,64,512]{4,3,2,1,0:T(8,128)(2,1)} %side.1, f32[2,64,256]{2,1,0:T(8,128)} %inlet.1, bf16[2,1,4,512,256]{4,3,2,1,0:T(8,128)(2,1)} %prev.1, ...), custom_call_target="tpu_custom_call" | custom-call | tf_op jit(solution)/shard_map/pallas_call | solution.py:477
  50.5 3.0 %copy.10 = bf16[2,1,4,512,256]{4,3,2,1,0:T(8,128)(2,1)} copy(bf16[2,1,4,512,256]{4,3,2,1,0:T(8,128)(2,1)} %shard_map.82) | data formatting | bytes 4194304

commit v2 on v1

--- a/solution.py
+++ b/solution.py
@@ -36,8 +36,8 @@
 
 
 def kernel(
-    order, inv, up, side, inlet, prev, upt, aff, out,
-    A, UL, PV, MN, F, SRC, LS, LR, LAT, H, G, INF, TT, TP, TC, THL, VV,
+    order_in, inv, up, side, inlet_in, prev, upt_in, aff_in, out,
+    order, inlet, upt, aff, A, UL, PV, MM, NN, MT, F, SRC, LS, LR, LAT, H, G, INF, TT, TP, TC, THL, VV,
     OS, OR, OC, X8S, X8R, YSND, XIN,
     ld_sem, lat_s, lat_r, t_s, t_r, tc_s, tc_r, s1_s, s1_r, s2_s, s2_r, z_s, z_r, s4_s, s4_r,
 ):
@@ -66,21 +66,37 @@
         loads[name] = c
 
     load("prev1", 0, prev.at[1, 0], PV.at[1])
-    load("u0", 2, up.at[0, 0], UL.at[0, :, 0:face])
-    load("l0", 4, side.at[0, 0], UL.at[0, :, face:])
-    load("al0", 6, inv.at[0, 0, :, edge:], A.at[0, :, edge:])
-    load("u1", 3, up.at[1, 0], UL.at[1, :, 0:face])
-    load("l1", 5, side.at[1, 0], UL.at[1, :, face:])
-    load("al1", 7, inv.at[1, 0, :, edge:], A.at[1, :, edge:])
-    load("prev0", 1, prev.at[0, 0], PV.at[0])
-    load("ar1", 9, inv.at[1, 0, :, 0:edge], A.at[1, :, 0:edge])
-    load("ar0", 8, inv.at[0, 0, :, 0:edge], A.at[0, :, 0:edge])
+    for c in (1, 0):
+        for k in range(2):
+            load(f"u{c}{k}", 2 + 2 * c + k, up.at[c, 0], UL.at[c, :, k * face : (k + 1) * face])
+            load(f"l{c}{k}", 6 + 2 * c + k, side.at[c, 0], UL.at[c, :, (2 + k) * face : (3 + k) * face])
+        load(f"al{c}", 10 + c, inv.at[c, 0, :, edge:], A.at[c, :, edge:])
+        if c:
+            load("order", 14, order_in, order)
+            load("upt", 15, upt_in, upt)
+            load("aff", 16, aff_in, aff)
+            load("prev0", 1, prev.at[0, 0], PV.at[0])
+    load("inlet", 17, inlet_in, inlet)
+    load("ar1", 13, inv.at[1, 0, :, 0:edge], A.at[1, :, 0:edge])
+    load("ar0", 12, inv.at[0, 0, :, 0:edge], A.at[0, :, 0:edge])
 
     barrier = pltpu.get_barrier_semaphore()
-    peers = [partner, ypeer(1), ypeer(2), ypeer(3), zpeer]
-    peers += [{"lat": lax.rem(lat + 1, lats)}, {"lat": lax.rem(lat + lats - 1, lats)}]
-    for peer in peers:
+
+    def hello(peer):
         pl.semaphore_signal(barrier, inc=1, device_id=peer, device_id_type=MESH)
+
+    for peer in (partner, ypeer(1), ypeer(2), ypeer(3)):
+        hello(peer)
+
+    @pl.when(lat > 0)
+    def _():
+        hello({"lat": lat - 1})
+
+    @pl.when(zhi == 1)
+    def _():
+        hello(zpeer)
+
+    expected = 4 + jnp.where(lat < lats - 1, 1, 0) + jnp.where(zhi == 0, 1, 0)
 
     def remote(src, dst, ssem, rsem, peer):
         return pltpu.make_async_remote_copy(
@@ -105,36 +121,44 @@
     def value_trace(x):
         return cat0(*[x[a * 64 + 56 : a * 64 + 64] for a in range(8)])
 
+    def apply(m4, h, l):
+        return dot(m4, cat0(h, l, h, l))
+
+    def put_maps(c, j, rows_of):
+        hi, lo = split(dot_nt(A[c, j, rows_of, :], UL[c, j]))
+        MM[c, j, rows_of, 0:128] = hi[:, 0:128]
+        MM[c, j, rows_of, 128:256] = lo[:, 0:128]
+        NN[c, j, rows_of, 0:128] = hi[:, 128:256]
+        NN[c, j, rows_of, 128:256] = lo[:, 128:256]
+
+    def edge_maps(c):
+        for n in (f"u{c}0", f"u{c}1", f"l{c}0", f"l{c}1", f"al{c}"):
+            loads[n].wait()
+        for j in range(rows):
+            put_maps(c, j, slice(edge, nodes))
+
     loads["prev1"].wait()
     for j in range(rows):
         LS[0, j] = prev_trace(1, j)
-    pl.semaphore_wait(barrier, len(peers))
+    edge_maps(1)
+    pl.semaphore_wait(barrier, expected)
     lat_send(0)
 
+    edge_maps(0)
+    loads["order"].wait()
+
+    def mm_edge(c, j):
+        return MM[c, j, edge:, :]
+
     for c in range(cols):
-        for n in ("u", "l", "al"):
-            loads[n + str(c)].wait()
-        for j in range(rows):
-            hi, lo = split(dot_nt(A[c, j, edge:, :], UL[c, j]))
-            MN[c, j, edge:, 0:128] = hi
-            MN[c, j, edge:, 128:256] = lo
-
-    def mn_edge(c, j):
-        return MN[c, j, edge:, :]
-
-    def apply(mn4, rh, rl):
-        return dot(mn4, cat0(rh, rh)) + dot(mn4[:, 0:128], rl)
-
-    zero64 = jnp.zeros((face, face), BF16)
-    for c in range(cols):
-        first = mn_edge(c, order[c, 0, 0])
+        first = mm_edge(c, order[c, 0, 0])
         g = first[:, 0:face].astype(F32) + first[:, 128 : 128 + face].astype(F32)
         for p in range(1, rows + 1):
-            gh, gl = split(g)
             if p < rows:
+                gh, gl = split(g)
                 G[c, 0, (p - 1) * face : p * face, :] = gh
                 G[c, 1, (p - 1) * face : p * face, :] = gl
-                g = apply(mn_edge(c, order[c, 0, p]), cat0(gh, zero64), cat0(gl, zero64))
+                g = apply(mm_edge(c, order[c, 0, p]), gh, gl)
         TT[c] = g
     t_copy = remote(TT, TP, t_s, t_r, partner)
     t_copy.start()
@@ -143,6 +167,9 @@
     for j in range(rows):
         LAT[0, 1, j] = prev_trace(0, j).astype(BF16)
         LAT[1, 1, j] = jnp.zeros((face, 256), BF16)
+    loads["inlet"].wait()
+    loads["upt"].wait()
+    loads["aff"].wait()
     for c in range(cols):
         piece = jnp.where(is0, inlet[c, :, 0:half], inlet[c, :, half:])
         piece = jnp.where(zhi == 0, piece, jnp.zeros_like(piece))
@@ -152,8 +179,11 @@
     rate = upt[...].reshape(1, 256)
     affinity = aff[...].reshape(1, 256)
 
+    inv_rate = 1.0 / rate
+    ratio = affinity * inv_rate
+
     def source_of(x):
-        return rate * x / (1.0 + affinity * jnp.abs(x))
+        return x / (inv_rate + ratio * jnp.abs(x))
 
     def put_source(c, j, x):
         hi, lo = split(source_of(x))
@@ -163,28 +193,21 @@
         F[c, j, edge:, :] = dot(a, hi) + dot(a, lo)
 
     def first_source(c):
-        def body(j, _):
+        for j in range(rows):
             put_source(c, j, PV[c, j].astype(F32))
-            return 0
-
-        lax.fori_loop(0, rows, body, 0)
-
-    def rest(c):
-        def body(j, _):
+
+    def rest(c, js):
+        for j in js:
             a = A[c, j, 0:edge, :]
-            F[c, j, 0:edge, :] = dot(a, SRC[c, 0, j]) + dot(a, SRC[c, 1, j])
-            return 0
-
-        lax.fori_loop(0, rows, body, 0)
+            side_part = apply(NN[c, j, 0:edge, :], LAT[0, c, j], LAT[1, c, j])
+            F[c, j, 0:edge, :] = dot(a, SRC[c, 0, j]) + dot(a, SRC[c, 1, j]) + side_part
 
     def maps_rest(c):
-        def body(j, _):
-            hi, lo = split(dot_nt(A[c, j, 0:edge, :], UL[c, j]))
-            MN[c, j, 0:edge, 0:128] = hi
-            MN[c, j, 0:edge, 128:256] = lo
-            return 0
-
-        lax.fori_loop(0, rows, body, 0)
+        for j in range(rows):
+            put_maps(c, j, slice(0, edge))
+            if c == 1:
+                parts = [MM[c, j, a * 64 + 48 : a * 64 + 64, :].astype(F32)[8:16] for a in range(8)]
+                MT[j] = cat0(*parts).astype(BF16)
 
     zero_trace = jnp.zeros((face, 256), BF16)
 
@@ -192,16 +215,14 @@
         return remote(OS.at[it, c, 1 - core], OR.at[it, c], s1_s.at[it, c], s1_r.at[it, c], partner)
 
     def chain(it, c):
-        drive = []
-        for p in range(rows):
-            j = order[c, 0, p]
-            lh, ll = LAT[0, c, j], LAT[1, c, j]
-            drive.append(F[c, j, edge:, :] + apply(mn_edge(c, j), cat0(zero_trace, lh), cat0(zero_trace, ll)))
-        h = drive[0]
+        for j in range(rows):
+            F[c, j, edge:, :] += apply(NN[c, j, edge:, :], LAT[0, c, j], LAT[1, c, j])
+        h = F[c, order[c, 0, 0], edge:, :]
         for p in range(1, rows):
             H[c, p - 1] = h
             hh, hl = split(h)
-            h = drive[p] + apply(mn_edge(c, order[c, 0, p]), cat0(hh, zero_trace), cat0(hl, zero_trace))
+            j = order[c, 0, p]
+            h = F[c, j, edge:, :] + apply(mm_edge(c, j), hh, hl)
         OS[it, c, 0] = h[:, 0:half]
         OS[it, c, 1] = h[:, half:]
         s1_copy(it, c).start()
@@ -287,31 +308,26 @@
 
     def solved(c, j):
         rank = rank_of(c, j)
-        rh = cat0(INF[0, c, rank], LAT[0, c, j])
-        rl = cat0(INF[1, c, rank], LAT[1, c, j])
-        return F[c, j] + apply(MN[c, j], rh, rl)
+        return F[c, j] + apply(MM[c, j], INF[0, c, rank], INF[1, c, rank])
+
+    def traces_ahead():
+        for j in range(rows):
+            rank = rank_of(1, j)
+            base = cat0(*[F[1, j, a * 64 + 56 : a * 64 + 64, :] for a in range(8)])
+            LS[1, j] = base + apply(MT[j], INF[0, 1, rank], INF[1, 1, rank])
 
     def lag(c):
-        def body(j, _):
+        for j in range(rows):
             x = solved(c, j)
-            trace = value_trace(x)
-            if c == 1:
-                LS[1, j] = trace
-            else:
-                hi, lo = split(trace)
+            if c == 0:
+                hi, lo = split(value_trace(x))
                 LAT[0, 1, j] = hi
                 LAT[1, 1, j] = lo
             put_source(c, j, x)
-            return 0
-
-        lax.fori_loop(0, rows, body, 0)
 
     def finish(c):
-        def body(j, _):
+        for j in range(rows):
             out[c, 0, j] = solved(c, j).astype(BF16)
-            return 0
-
-        lax.fori_loop(0, rows, body, 0)
 
     def lat_arrival(it):
         @pl.when(lat > 0)
@@ -351,6 +367,8 @@
     chain(0, 1)
     first_source(0)
     compose(0, 1)
+    loads["ar1"].wait()
+    maps_rest(1)
 
     for d in (1, 3, 2):
         tc_arrival(d).wait_recv()
@@ -377,32 +395,55 @@
         VV[c, 0] = vh
         VV[c, 1] = vl
 
+    early, late = range(0, 2), range(2, rows)
     lat_arrival(0)
     chain(0, 0)
-    loads["ar1"].wait()
-    maps_rest(1)
+    gather(0, 1)
+    rest(1, early)
     compose(0, 0)
-    rest(1)
-    gather(0, 1)
+    rest(1, late)
     loads["ar0"].wait()
     maps_rest(0)
-    rest(0)
+    rest(0, range(rows))
     gather(0, 0)
     carry(0, 1)
     inflows(0, 1)
+    traces_ahead()
+    lat_send(1)
     lag(1)
-    lat_send(1)
     carry(0, 0)
     inflows(0, 0)
     lag(0)
 
     chain(1, 1)
-    rest(1)
-    compose(1, 1)
     lat_arrival(1)
     chain(1, 0)
-    rest(0)
+    rest(1, early)
+    compose(1, 1)
     compose(1, 0)
+    rest(1, late)
+    rest(0, range(rows))
+
+    def sent(it):
+        for c in range(cols):
+            s1_copy(it, c).wait_send()
+            s4_copy(it, c).wait_send()
+            for d in range(1, YS):
+                s2_copy(it, c, d).wait_send()
+
+        @pl.when(zhi == 0)
+        def _():
+            for c in range(cols):
+                z_copy(it, c).wait_send()
+
+        @pl.when(lat < lats - 1)
+        def _():
+            lat_copy(it).wait_send()
+
+    t_copy.wait_send()
+    for d in range(1, YS):
+        tc_copy(d).wait_send()
+    sent(0)
     gather(1, 1)
     carry(1, 1)
     gather(1, 0)
@@ -411,24 +452,7 @@
     finish(1)
     inflows(1, 0)
     finish(0)
-
-    t_copy.wait_send()
-    for d in range(1, YS):
-        tc_copy(d).wait_send()
-    for it in range(2):
-        for c in range(cols):
-            s1_copy(it, c).wait_send()
-            s4_copy(it, c).wait_send()
-            for d in range(1, YS):
-                s2_copy(it, c, d).wait_send()
-
-            @pl.when(zhi == 0)
-            def _():
-                z_copy(it, c).wait_send()
-
-        @pl.when(lat < lats - 1)
-        def _():
-            lat_copy(it).wait_send()
+    sent(1)
 
 
 def cat_lanes(t, width):
@@ -437,14 +461,21 @@
 
 
 def per_device(inverse, upwind, lateral, inlet_trace, previous, uptake_rate, affinity, flow_order):
-    any_space = pl.BlockSpec(memory_space=pltpu.HBM)
+    operands = (flow_order, inverse, upwind, lateral, inlet_trace, previous, uptake_rate, affinity)
+    hbm = pl.BlockSpec(memory_space=pltpu.HBM)
     vmem = pl.BlockSpec(memory_space=pltpu.VMEM)
     dma = pltpu.SemaphoreType.DMA
     scratch = [
+        pltpu.SMEM((2, 1, 4), jnp.int32),
+        pltpu.VMEM((2, 64, 256), F32),
+        pltpu.VMEM((256,), F32),
+        pltpu.VMEM((256,), F32),
         pltpu.VMEM((2, 4, 512, 512), BF16),
-        pltpu.VMEM((2, 4, 128, 512), BF16),
+        pltpu.VMEM((2, 4, 256, 512), BF16),
         pltpu.VMEM((2, 4, 512, 256), BF16),
         pltpu.VMEM((2, 4, 512, 256), BF16),
+        pltpu.VMEM((2, 4, 512, 256), BF16),
+        pltpu.VMEM((4, 64, 256), BF16),
         pltpu.VMEM((2, 4, 512, 256), F32),
         pltpu.VMEM((2, 2, 4, 512, 256), BF16),
         pltpu.VMEM((2, 4, 64, 256), F32),
@@ -465,7 +496,7 @@
         pltpu.VMEM((2, 2, 64, 128), F32),
         pltpu.VMEM((2, 2, 64, 128), F32),
         pltpu.VMEM((2, 2, 2, 64, 128), F32),
-        dma((10,)),
+        dma((18,)),
         dma((2,)), dma((2,)),
         dma, dma,
         dma((3,)), dma((4,)),
@@ -477,16 +508,13 @@
     return pl.pallas_call(
         kernel,
         out_shape=jax.ShapeDtypeStruct(previous.shape, BF16),
-        in_specs=[
-            pl.BlockSpec(memory_space=pltpu.SMEM),
-            any_space, any_space, any_space, vmem, any_space, vmem, vmem,
-        ],
+        in_specs=[hbm] * 8,
         out_specs=vmem,
         scratch_shapes=scratch,
         compiler_params=pltpu.CompilerParams(
-            collective_id=0, has_side_effects=True, vmem_limit_bytes=60 * 1024 * 1024
+            collective_id=0, has_side_effects=True, vmem_limit_bytes=40 * 1024 * 1024
         ),
-    )(flow_order, inverse, upwind, lateral, inlet_trace, previous, uptake_rate, affinity)
+    )(*(pltpu.with_memory_space_constraint(a, pltpu.HBM) for a in operands))
 
 
 def solution(mesh):

time: 53.7 us -> 46.7 us (0.87)
  Pallas kernels: 50.4 us -> 45.3 us
  local copies, waits for them, and re-layouts: 3.05 us -> 1.32 us
    pallas_call x1, Pallas kernels: 50.4 us -> 45.3 us  [per_device(): pl.pallas_call(kernel, out_shape=jax.ShapeDtypeStruct(previous.shape, BF1...]
    unnamed x1, local copies, waits for them, and re-layouts: 3.05 us -> 1.32 us
where the time goes in v2:
time: 46.7 us
  Pallas kernels  45.3 us (97%)
  local copies, waits for them, and re-layouts  1.32 us (3%)
    pallas_call x1, Pallas kernels, per_device(): pl.pallas_call(kernel, out_shape=jax.ShapeDtypeStruct(previous.shape, BF1...  45.3 us
    unnamed x1, local copies, waits for them, and re-layouts  1.32 us

profile of v2, /device:TPU:225, one launch (start us, length us, event | category | flops | bytes accessed | tf_op | source)
XLA Modules:
  0.0 46.7 jit_solution(4199256511388284542)
XLA Ops:
  0.0 45.3 %shard_map.82 = bf16[2,1,4,512,256]{4,3,2,1,0:T(8,128)(2,1)S(1)} custom-call(s32[2,1,4]{2,1,0:T(1,128)} %order_in.1, bf16[2,1,4,512,512]{4,3,2,1,0:T(8,128)(2,1)} %inv.1, bf16[2,1,4,64,512]{4,3,2,1,0:T(8,128)(2,1)} %up.1, bf16[2,1,4,64,512]{4,3,2,1,0:T(8,128)(2,1)} %side.1, f32[2,64,256]{2,1,0:T(8,128)} %inlet_in.1, bf16[2,1,4,512,256]{4,3,2,1,0:T(8,128)(2,1)} %prev.1, ...), custom_call_target="tpu_custom_call" | custom-call | tf_op jit(solution)/shard_map/pallas_call | solution.py:508
  45.3 1.3 %copy.10 = bf16[2,1,4,512,256]{4,3,2,1,0:T(8,128)(2,1)} copy(bf16[2,1,4,512,256]{4,3,2,1,0:T(8,128)(2,1)S(1)} %shard_map.82) | data formatting | bytes 4194304

commit v3 on v2

--- a/solution.py
+++ b/solution.py
@@ -37,9 +37,9 @@
 
 def kernel(
     order_in, inv, up, side, inlet_in, prev, upt_in, aff_in, out,
-    order, inlet, upt, aff, A, UL, PV, MM, NN, MT, F, SRC, LS, LR, LAT, H, G, INF, TT, TP, TC, THL, VV,
-    OS, OR, OC, X8S, X8R, YSND, XIN,
-    ld_sem, lat_s, lat_r, t_s, t_r, tc_s, tc_r, s1_s, s1_r, s2_s, s2_r, z_s, z_r, s4_s, s4_r,
+    order, inlet, upt, aff, A, UL, PV, MM, NN, F, SRC, LS, LR, LAT, H, G, INF, TT, TP, TC, THL, VV,
+    OS, OR, OC, X8S, X8R, YSND, XIN, VO, XE, XL, RS, RR,
+    ld_sem, lat_s, lat_r, t_s, t_r, tc_s, tc_r, s1_s, s1_r, s2_s, s2_r, z_s, z_r, s4_s, s4_r, x_s, x_r, r_s, r_r, ready,
 ):
     cols, rows, nodes, face = 2, 4, 512, 64
     half = 128
@@ -56,7 +56,12 @@
     def ypeer(d):
         return {"stream": zhi * (2 * YS) + lax.rem(y + d, YS) * 2 + core}
 
-    zpeer = {"stream": lax.rem(s + 2 * YS, 4 * YS)}
+
+    def above(k):
+        return {"stream": 2 * YS + 2 * y + k}
+
+    def below(k):
+        return {"stream": 2 * y + k}
 
     loads = {}
 
@@ -75,7 +80,7 @@
             load("order", 14, order_in, order)
             load("upt", 15, upt_in, upt)
             load("aff", 16, aff_in, aff)
-            load("prev0", 1, prev.at[0, 0], PV.at[0])
+    load("prev0", 1, prev.at[0, 0], PV.at[0])
     load("inlet", 17, inlet_in, inlet)
     load("ar1", 13, inv.at[1, 0, :, 0:edge], A.at[1, :, 0:edge])
     load("ar0", 12, inv.at[0, 0, :, 0:edge], A.at[0, :, 0:edge])
@@ -92,11 +97,12 @@
     def _():
         hello({"lat": lat - 1})
 
-    @pl.when(zhi == 1)
+    @pl.when(zhi == 0)
     def _():
-        hello(zpeer)
-
-    expected = 4 + jnp.where(lat < lats - 1, 1, 0) + jnp.where(zhi == 0, 1, 0)
+        hello(above(0))
+        hello(above(1))
+
+    expected = 4 + jnp.where(lat < lats - 1, 1, 0) + jnp.where(zhi == 1, 2, 0)
 
     def remote(src, dst, ssem, rsem, peer):
         return pltpu.make_async_remote_copy(
@@ -140,24 +146,35 @@
     loads["prev1"].wait()
     for j in range(rows):
         LS[0, j] = prev_trace(1, j)
-    edge_maps(1)
     pl.semaphore_wait(barrier, expected)
     lat_send(0)
 
+    @pl.when(zhi == 1)
+    def _():
+        for k in range(2):
+            pl.semaphore_signal(ready, inc=1, device_id=below(k), device_id_type=MESH)
+
+    edge_maps(1)
+
     edge_maps(0)
     loads["order"].wait()
 
     def mm_edge(c, j):
         return MM[c, j, edge:, :]
 
+    eye_row = lax.broadcasted_iota(jnp.int32, (face, face), 0)
+    eye_lane = lax.broadcasted_iota(jnp.int32, (face, face), 1)
+    eye = jnp.where(eye_row == eye_lane, 1.0, 0.0).astype(BF16)
     for c in range(cols):
+        G[c, 0, 0] = eye
+        G[c, 1, 0] = jnp.zeros((face, face), BF16)
         first = mm_edge(c, order[c, 0, 0])
         g = first[:, 0:face].astype(F32) + first[:, 128 : 128 + face].astype(F32)
         for p in range(1, rows + 1):
             if p < rows:
                 gh, gl = split(g)
-                G[c, 0, (p - 1) * face : p * face, :] = gh
-                G[c, 1, (p - 1) * face : p * face, :] = gl
+                G[c, 0, p] = gh
+                G[c, 1, p] = gl
                 g = apply(mm_edge(c, order[c, 0, p]), gh, gl)
         TT[c] = g
     t_copy = remote(TT, TP, t_s, t_r, partner)
@@ -205,9 +222,6 @@
     def maps_rest(c):
         for j in range(rows):
             put_maps(c, j, slice(0, edge))
-            if c == 1:
-                parts = [MM[c, j, a * 64 + 48 : a * 64 + 64, :].astype(F32)[8:16] for a in range(8)]
-                MT[j] = cat0(*parts).astype(BF16)
 
     zero_trace = jnp.zeros((face, 256), BF16)
 
@@ -245,18 +259,17 @@
         for d in (2, 1, 3):
             s2_copy(it, c, d).start()
 
-    def z_copy(it, c):
-        return remote(X8S.at[it, c], X8R.at[it, c], z_s.at[it, c], z_r.at[it, c], zpeer)
+    def z_copy(it, c, k):
+        return remote(X8S.at[it, c], X8R.at[it, c, core], z_s.at[it, c, k], z_r.at[it, c, core], above(k))
+
+    def z_arrival(it, c, h):
+        return remote(X8S.at[it, c], X8R.at[it, c, h], z_s.at[it, c, h], z_r.at[it, c, h], partner)
 
     def s4_copy(it, c):
         return remote(YSND.at[it, c], XIN.at[it, c, core], s4_s.at[it, c], s4_r.at[it, c], partner)
 
     def s4_arrival(it, c):
         return remote(YSND.at[it, c], XIN.at[it, c, 1 - core], s4_s.at[it, c], s4_r.at[it, c], partner)
-
-    def put_entering(it, c, q):
-        YSND[it, c] = jnp.where(is0, q[face:], q[0:face])
-        XIN[it, c, core] = jnp.where(is0, q[0:face], q[face:])
 
     def gather(it, c):
         for d in (1, 3, 2):
@@ -264,37 +277,50 @@
         offsets = OC[it, c].reshape((YS + 1) * face, half)
         q = dot3(VV[c, 0], VV[c, 1], offsets)
         o_first, _ = first_second(it, c)
-        q = cat0(q[0:face], q[face : 2 * face] + o_first, q[2 * face :])
+        first, second = q[0:face], q[face : 2 * face] + o_first
 
         @pl.when(zhi == 0)
         def _():
             X8S[it, c] = q[2 * face :]
-            z_copy(it, c).start()
-            put_entering(it, c, q[0 : 2 * face])
-            s4_copy(it, c).start()
+            if it == 0 and c == 1:
+                pl.semaphore_wait(ready, 2)
+            for k in range(2):
+                z_copy(it, c, k).start()
+
+        YSND[it, c] = jnp.where(is0, second, first)
+        XIN[it, c, core] = jnp.where(is0, first, second)
+        s4_copy(it, c).start()
+
+    def x_copy():
+        return remote(XE.at[0, 1], XL, x_s, x_r, {"lat": lax.rem(lat + 1, lats)})
+
+    def r_copy():
+        return remote(RS, RR, r_s, r_r, {"lat": lax.rem(lat + 1, lats)})
+
+    def enter(it, c):
+        s4_arrival(it, c).wait_recv()
+        XE[it, c] = jnp.concatenate([XIN[it, c, 0], XIN[it, c, 1]], axis=1)
 
         @pl.when(zhi == 1)
         def _():
-            X8S[it, c] = q[0:face]
-            YSND[it, c] = q[face : 2 * face]
-
-    def carry(it, c):
-        @pl.when(zhi == 1)
-        def _():
-            z_copy(it, c).wait_recv()
-            q = cat0(X8S[it, c], YSND[it, c])
-            v = slice(YS * face, (YS + 1) * face)
-            q = q + dot3(VV[c, 0, 0 : 2 * face, v], VV[c, 1, 0 : 2 * face, v], X8R[it, c])
-            put_entering(it, c, q)
-            s4_copy(it, c).start()
+            for h in range(2):
+                z_arrival(it, c, h).wait_recv()
+            carried = jnp.concatenate([X8R[it, c, 0], X8R[it, c, 1]], axis=1)
+            XE[it, c] += dot3(VO[c, 0], VO[c, 1], carried)
+
+        if it == 0 and c == 1:
+
+            @pl.when(lat < lats - 1)
+            def _():
+                x_copy().start()
 
     def inflows(it, c):
-        s4_arrival(it, c).wait_recv()
-        x = jnp.concatenate([XIN[it, c, 0], XIN[it, c, 1]], axis=1)
-        xh, xl = split(x)
+        xh, xl = split(XE[it, c])
         INF[0, c, 0] = xh
         INF[1, c, 0] = xl
-        later = dot(G[c, 0], xh) + (dot(G[c, 1], xh) + dot(G[c, 0], xl))
+        gh = G[c, 0, 1:].reshape((rows - 1) * face, face)
+        gl = G[c, 1, 1:].reshape((rows - 1) * face, face)
+        later = dot(gh, xh) + (dot(gl, xh) + dot(gh, xl))
         for p in range(1, rows):
             xh, xl = split(later[(p - 1) * face : p * face] + H[c, p - 1])
             INF[0, c, p] = xh
@@ -312,9 +338,20 @@
 
     def traces_ahead():
         for j in range(rows):
+            a = cat0(*[A[1, j, i * 64 + 48 : i * 64 + 64, :].astype(F32)[8:16] for i in range(8)]).astype(BF16)
+            hi, lo = split(dot_nt(a, UL[1, j]))
+            mt = jnp.concatenate([hi[:, 0:128], lo[:, 0:128]], axis=1)
+            nt = jnp.concatenate([hi[:, 128:256], lo[:, 128:256]], axis=1)
             rank = rank_of(1, j)
-            base = cat0(*[F[1, j, a * 64 + 56 : a * 64 + 64, :] for a in range(8)])
-            LS[1, j] = base + apply(MT[j], INF[0, 1, rank], INF[1, 1, rank])
+            hh, hl = split(jnp.where(rank > 0, H[1, jnp.maximum(rank - 1, 0)], 0.0))
+            base = dot(a, SRC[1, 0, j]) + dot(a, SRC[1, 1, j])
+            LS[1, j] = base + apply(nt, LAT[0, 1, j], LAT[1, 1, j]) + apply(mt, hh, hl)
+            RS[j] = apply(mt, G[1, 0, rank], G[1, 1, rank])
+
+        @pl.when(lat < lats - 1)
+        def _():
+            r_copy().start()
+            lat_copy(1).start()
 
     def lag(c):
         for j in range(rows):
@@ -333,8 +370,16 @@
         @pl.when(lat > 0)
         def _():
             lat_copy(it).wait_recv()
+            if it == 1:
+                r_copy().wait_recv()
+                x_copy().wait_recv()
+                xh, xl = split(XL[...])
             for j in range(rows):
-                hi, lo = split(LR[it, j])
+                trace = LR[it, j]
+                if it == 1:
+                    rh, rl = split(RR[j])
+                    trace = trace + (dot(rh, xh) + (dot(rl, xh) + dot(rh, xl)))
+                hi, lo = split(trace)
                 LAT[0, 0, j] = hi
                 LAT[1, 0, j] = lo
 
@@ -343,6 +388,35 @@
             for j in range(rows):
                 LAT[0, 0, j] = zero_trace
                 LAT[1, 0, j] = zero_trace
+
+    def prefix_maps():
+        for d in (1, 3, 2):
+            tc_arrival(d).wait_recv()
+        width = (YS + 1) * face
+        row_id = lax.broadcasted_iota(jnp.int32, (face, width), 0)
+        lane_id = lax.broadcasted_iota(jnp.int32, (face, width), 1)
+
+        def unit(block):
+            return jnp.where(lane_id - face * block == row_id, 1.0, 0.0).astype(F32)
+
+        for c in range(cols):
+            x = unit(YS)
+            mine = jnp.where(y == 0, x, jnp.zeros_like(x))
+            for t in range(YS):
+                if t == 0:
+                    x = cat_lanes(TC[0, c], width) + unit(0)
+                else:
+                    th, tl = split(TC[t, c])
+                    x = dot3(th, tl, x) + unit(t)
+                if t + 1 < YS:
+                    mine = jnp.where(y == t + 1, x, mine)
+            both = dot3(THL[0, c, 0], THL[0, c, 1], mine)
+            vh, vl = split(cat0(mine, both, x))
+            VV[c, 0] = vh
+            VV[c, 1] = vl
+            v = slice(YS * face, (YS + 1) * face)
+            VO[c, 0] = jnp.where(is0, vh[0:face, v], vh[face : 2 * face, v])
+            VO[c, 1] = jnp.where(is0, vl[0:face, v], vl[face : 2 * face, v])
 
     first_source(1)
 
@@ -368,61 +442,47 @@
     first_source(0)
     compose(0, 1)
     loads["ar1"].wait()
+    traces_ahead()
     maps_rest(1)
-
-    for d in (1, 3, 2):
-        tc_arrival(d).wait_recv()
-    width = (YS + 1) * face
-    row_id = lax.broadcasted_iota(jnp.int32, (face, width), 0)
-    lane_id = lax.broadcasted_iota(jnp.int32, (face, width), 1)
-
-    def unit(block):
-        return jnp.where(lane_id - face * block == row_id, 1.0, 0.0).astype(F32)
-
-    for c in range(cols):
-        x = unit(YS)
-        mine = jnp.where(y == 0, x, jnp.zeros_like(x))
-        for t in range(YS):
-            if t == 0:
-                x = cat_lanes(TC[0, c], width) + unit(0)
-            else:
-                th, tl = split(TC[t, c])
-                x = dot3(th, tl, x) + unit(t)
-            if t + 1 < YS:
-                mine = jnp.where(y == t + 1, x, mine)
-        both = dot3(THL[0, c, 0], THL[0, c, 1], mine)
-        vh, vl = split(cat0(mine, both, x))
-        VV[c, 0] = vh
-        VV[c, 1] = vl
 
     early, late = range(0, 2), range(2, rows)
     lat_arrival(0)
     chain(0, 0)
-    gather(0, 1)
     rest(1, early)
     compose(0, 0)
+    prefix_maps()
+    gather(0, 1)
     rest(1, late)
+
+    @pl.when(zhi == 0)
+    def _():
+        enter(0, 1)
+
     loads["ar0"].wait()
     maps_rest(0)
-    rest(0, range(rows))
+    rest(0, early)
     gather(0, 0)
-    carry(0, 1)
+    rest(0, late)
+
+    @pl.when(zhi == 1)
+    def _():
+        enter(0, 1)
+
     inflows(0, 1)
-    traces_ahead()
-    lat_send(1)
     lag(1)
-    carry(0, 0)
+    enter(0, 0)
     inflows(0, 0)
     lag(0)
-
+    lat_arrival(1)
+
+    chain(1, 0)
     chain(1, 1)
-    lat_arrival(1)
-    chain(1, 0)
-    rest(1, early)
+    rest(0, range(0, 1))
+    compose(1, 0)
+    rest(0, range(1, 2))
     compose(1, 1)
-    compose(1, 0)
-    rest(1, late)
-    rest(0, range(rows))
+    rest(0, late)
+    rest(1, range(rows))
 
     def sent(it):
         for c in range(cols):
@@ -434,7 +494,8 @@
         @pl.when(zhi == 0)
         def _():
             for c in range(cols):
-                z_copy(it, c).wait_send()
+                for k in range(2):
+                    z_copy(it, c, k).wait_send()
 
         @pl.when(lat < lats - 1)
         def _():
@@ -443,15 +504,21 @@
     t_copy.wait_send()
     for d in range(1, YS):
         tc_copy(d).wait_send()
+
+    @pl.when(lat < lats - 1)
+    def _():
+        x_copy().wait_send()
+        r_copy().wait_send()
+
     sent(0)
+    gather(1, 0)
     gather(1, 1)
-    carry(1, 1)
-    gather(1, 0)
-    carry(1, 0)
+    enter(1, 0)
+    inflows(1, 0)
+    finish(0)
+    enter(1, 1)
     inflows(1, 1)
     finish(1)
-    inflows(1, 0)
-    finish(0)
     sent(1)
 
 
@@ -475,14 +542,13 @@
         pltpu.VMEM((2, 4, 512, 256), BF16),
         pltpu.VMEM((2, 4, 512, 256), BF16),
         pltpu.VMEM((2, 4, 512, 256), BF16),
-        pltpu.VMEM((4, 64, 256), BF16),
         pltpu.VMEM((2, 4, 512, 256), F32),
         pltpu.VMEM((2, 2, 4, 512, 256), BF16),
         pltpu.VMEM((2, 4, 64, 256), F32),
         pltpu.VMEM((2, 4, 64, 256), F32),
         pltpu.VMEM((2, 2, 4, 64, 256), BF16),
         pltpu.VMEM((2, 3, 64, 256), F32),
-        pltpu.VMEM((2, 2, 192, 64), BF16),
+        pltpu.VMEM((2, 2, 4, 64, 64), BF16),
         pltpu.VMEM((2, 2, 4, 64, 256), BF16),
         pltpu.VMEM((2, 64, 64), F32),
         pltpu.VMEM((2, 64, 64), F32),
@@ -493,17 +559,24 @@
         pltpu.VMEM((2, 2, 64, 128), F32),
         pltpu.VMEM((2, 2, 5, 64, 128), F32),
         pltpu.VMEM((2, 2, 64, 128), F32),
-        pltpu.VMEM((2, 2, 64, 128), F32),
+        pltpu.VMEM((2, 2, 2, 64, 128), F32),
         pltpu.VMEM((2, 2, 64, 128), F32),
         pltpu.VMEM((2, 2, 2, 64, 128), F32),
+        pltpu.VMEM((2, 2, 64, 64), BF16),
+        pltpu.VMEM((2, 2, 64, 256), F32),
+        pltpu.VMEM((64, 256), F32),
+        pltpu.VMEM((4, 64, 64), F32),
+        pltpu.VMEM((4, 64, 64), F32),
         dma((18,)),
         dma((2,)), dma((2,)),
         dma, dma,
         dma((3,)), dma((4,)),
         dma((2, 2)), dma((2, 2)),
         dma((2, 2, 3)), dma((2, 2, 4)),
+        dma((2, 2, 2)), dma((2, 2, 2)),
         dma((2, 2)), dma((2, 2)),
-        dma((2, 2)), dma((2, 2)),
+        dma, dma, dma, dma,
+        pltpu.SemaphoreType.REGULAR,
     ]
     return pl.pallas_call(
         kernel,

time: 46.7 us -> 42.8 us (0.916)
  Pallas kernels: 45.3 us -> 41.4 us
    pallas_call x1, Pallas kernels: 45.3 us -> 41.4 us  [per_device(): pl.pallas_call(kernel, out_shape=jax.ShapeDtypeStruct(previous.shape, BF1...]
where the time goes in v3:
time: 42.8 us; the launch traced here: 42.7 us
  Pallas kernels  41.4 us (97%)
  local copies, waits for them, and re-layouts  1.32 us (3%)
    pallas_call x1, Pallas kernels, per_device(): pl.pallas_call(kernel, out_shape=jax.ShapeDtypeStruct(previous.shape, BF1...  41.4 us
    unnamed x1, local copies, waits for them, and re-layouts  1.32 us

profile of v3, /device:TPU:225, one launch (start us, length us, event | category | flops | bytes accessed | tf_op | source)
XLA Modules:
  0.0 42.7 jit_solution(1420555957755239233)
XLA Ops:
  0.0 41.4 %shard_map.82 = bf16[2,1,4,512,256]{4,3,2,1,0:T(8,128)(2,1)S(1)} custom-call(s32[2,1,4]{2,1,0:T(1,128)} %order_in.1, bf16[2,1,4,512,512]{4,3,2,1,0:T(8,128)(2,1)} %inv.1, bf16[2,1,4,64,512]{4,3,2,1,0:T(8,128)(2,1)} %up.1, bf16[2,1,4,64,512]{4,3,2,1,0:T(8,128)(2,1)} %side.1, f32[2,64,256]{2,1,0:T(8,128)} %inlet_in.1, bf16[2,1,4,512,256]{4,3,2,1,0:T(8,128)(2,1)} %prev.1, ...), custom_call_target="tpu_custom_call" | custom-call | tf_op jit(solution)/shard_map/pallas_call | solution.py:581
  41.4 1.3 %copy.10 = bf16[2,1,4,512,256]{4,3,2,1,0:T(8,128)(2,1)} copy(bf16[2,1,4,512,256]{4,3,2,1,0:T(8,128)(2,1)S(1)} %shard_map.82) | data formatting | bytes 4194304

commit v4 on v3

--- a/solution.py
+++ b/solution.py
@@ -38,8 +38,8 @@
 def kernel(
     order_in, inv, up, side, inlet_in, prev, upt_in, aff_in, out,
     order, inlet, upt, aff, A, UL, PV, MM, NN, F, SRC, LS, LR, LAT, H, G, INF, TT, TP, TC, THL, VV,
-    OS, OR, OC, X8S, X8R, YSND, XIN, VO, XE, XL, RS, RR,
-    ld_sem, lat_s, lat_r, t_s, t_r, tc_s, tc_r, s1_s, s1_r, s2_s, s2_r, z_s, z_r, s4_s, s4_r, x_s, x_r, r_s, r_r, ready,
+    OS, OR, OC, X8S, X8R, YSND, XIN, VO, XE, XL, RS, RR, RL,
+    ld_sem, lat_s, lat_r, t_s, t_r, tc_s, tc_r, s1_s, s1_r, s2_s, s2_r, z_s, z_r, s4_s, s4_r, x_s, x_r, r_s, r_r, rl_s, rl_r, ready,
 ):
     cols, rows, nodes, face = 2, 4, 512, 64
     half = 128
@@ -51,6 +51,10 @@
     y = lax.rem(s // 2, YS)
     zhi = s // (2 * YS)
     is0 = core == 0
+    xs = 4
+    bends = (lax.rem(lat, xs) == xs - 1) & (lat < lats - 1)
+    relays = (lax.rem(lat, xs) == 0) & (lat < lats - xs)
+    relayed = (lax.rem(lat, xs) == 0) & (lat > 0)
     partner = {"stream": s + 1 - 2 * core}
 
     def ypeer(d):
@@ -62,6 +66,34 @@
 
     def below(k):
         return {"stream": 2 * y + k}
+
+    barrier = pltpu.get_barrier_semaphore()
+
+    def hello(peer):
+        pl.semaphore_signal(barrier, inc=1, device_id=peer, device_id_type=MESH)
+
+    for peer in (partner, ypeer(1), ypeer(2), ypeer(3)):
+        hello(peer)
+
+    @pl.when(lat > 0)
+    def _():
+        hello({"lat": lat - 1})
+
+    @pl.when(relays)
+    def _():
+        hello({"lat": lat + xs - 1})
+
+    @pl.when(relayed)
+    def _():
+        hello({"lat": lat - xs})
+
+    @pl.when(zhi == 0)
+    def _():
+        hello(above(0))
+        hello(above(1))
+
+    expected = 4 + jnp.where(lat < lats - 1, 1, 0) + jnp.where(zhi == 1, 2, 0)
+    expected = expected + jnp.where(bends, 1, 0) + jnp.where(relays, 1, 0)
 
     loads = {}
 
@@ -84,25 +116,6 @@
     load("inlet", 17, inlet_in, inlet)
     load("ar1", 13, inv.at[1, 0, :, 0:edge], A.at[1, :, 0:edge])
     load("ar0", 12, inv.at[0, 0, :, 0:edge], A.at[0, :, 0:edge])
-
-    barrier = pltpu.get_barrier_semaphore()
-
-    def hello(peer):
-        pl.semaphore_signal(barrier, inc=1, device_id=peer, device_id_type=MESH)
-
-    for peer in (partner, ypeer(1), ypeer(2), ypeer(3)):
-        hello(peer)
-
-    @pl.when(lat > 0)
-    def _():
-        hello({"lat": lat - 1})
-
-    @pl.when(zhi == 0)
-    def _():
-        hello(above(0))
-        hello(above(1))
-
-    expected = 4 + jnp.where(lat < lats - 1, 1, 0) + jnp.where(zhi == 1, 2, 0)
 
     def remote(src, dst, ssem, rsem, peer):
         return pltpu.make_async_remote_copy(
@@ -337,6 +350,7 @@
         return F[c, j] + apply(MM[c, j], INF[0, c, rank], INF[1, c, rank])
 
     def traces_ahead():
+        maps = []
         for j in range(rows):
             a = cat0(*[A[1, j, i * 64 + 48 : i * 64 + 64, :].astype(F32)[8:16] for i in range(8)]).astype(BF16)
             hi, lo = split(dot_nt(a, UL[1, j]))
@@ -346,12 +360,48 @@
             hh, hl = split(jnp.where(rank > 0, H[1, jnp.maximum(rank - 1, 0)], 0.0))
             base = dot(a, SRC[1, 0, j]) + dot(a, SRC[1, 1, j])
             LS[1, j] = base + apply(nt, LAT[0, 1, j], LAT[1, 1, j]) + apply(mt, hh, hl)
-            RS[j] = apply(mt, G[1, 0, rank], G[1, 1, rank])
+            maps.append(apply(mt, G[1, 0, rank], G[1, 1, rank]))
+        for k in range(2):
+            RS[k] = jnp.concatenate([maps[2 * k], maps[2 * k + 1]], axis=1)
+
 
         @pl.when(lat < lats - 1)
         def _():
+            part_copy(0).start()
+
+        @pl.when((lat < lats - 1) & jnp.logical_not(bends))
+        def _():
+            part_copy(1).start()
             r_copy().start()
-            lat_copy(1).start()
+
+        @pl.when(bends)
+        def _():
+            bend_copy().start()
+
+    def map_send():
+        @pl.when(bends)
+        def _():
+            r_copy().start()
+
+    def part_copy(k):
+        js = pl.ds(2 * k, 2)
+        return remote(LS.at[1, js], LR.at[1, js], lat_s.at[1 + k], lat_r.at[1 + k], {"lat": lax.rem(lat + 1, lats)})
+
+    back = pl.ds(2, 2)
+
+    def bend_copy():
+        peer = {"lat": lax.rem(lat + lats - xs + 1, lats)}
+        return remote(LS.at[1, back], RL, lat_s.at[2], rl_r, peer)
+
+    def relay_copy():
+        peer = {"lat": lax.rem(lat + xs, lats)}
+        return remote(RL, LR.at[1, back], rl_s, lat_r.at[2], peer)
+
+    def pass_on():
+        @pl.when(relays)
+        def _():
+            bend_copy().wait_recv()
+            relay_copy().start()
 
     def lag(c):
         for j in range(rows):
@@ -369,15 +419,18 @@
     def lat_arrival(it):
         @pl.when(lat > 0)
         def _():
-            lat_copy(it).wait_recv()
-            if it == 1:
+            if it == 0:
+                lat_copy(it).wait_recv()
+            else:
+                for k in range(2):
+                    part_copy(k).wait_recv()
                 r_copy().wait_recv()
                 x_copy().wait_recv()
                 xh, xl = split(XL[...])
             for j in range(rows):
                 trace = LR[it, j]
                 if it == 1:
-                    rh, rl = split(RR[j])
+                    rh, rl = split(RR[j // 2][:, (j % 2) * face : (j % 2 + 1) * face])
                     trace = trace + (dot(rh, xh) + (dot(rl, xh) + dot(rh, xl)))
                 hi, lo = split(trace)
                 LAT[0, 0, j] = hi
@@ -452,6 +505,7 @@
     compose(0, 0)
     prefix_maps()
     gather(0, 1)
+    map_send()
     rest(1, late)
 
     @pl.when(zhi == 0)
@@ -469,6 +523,7 @@
         enter(0, 1)
 
     inflows(0, 1)
+    pass_on()
     lag(1)
     enter(0, 0)
     inflows(0, 0)
@@ -477,11 +532,9 @@
 
     chain(1, 0)
     chain(1, 1)
-    rest(0, range(0, 1))
     compose(1, 0)
-    rest(0, range(1, 2))
     compose(1, 1)
-    rest(0, late)
+    rest(0, range(rows))
     rest(1, range(rows))
 
     def sent(it):
@@ -499,7 +552,17 @@
 
         @pl.when(lat < lats - 1)
         def _():
-            lat_copy(it).wait_send()
+            if it == 0:
+                lat_copy(it).wait_send()
+            else:
+                for k in range(2):
+                    part_copy(k).wait_send()
+
+        if it == 1:
+
+            @pl.when(relays)
+            def _():
+                relay_copy().wait_send()
 
     t_copy.wait_send()
     for d in range(1, YS):
@@ -565,10 +628,11 @@
         pltpu.VMEM((2, 2, 64, 64), BF16),
         pltpu.VMEM((2, 2, 64, 256), F32),
         pltpu.VMEM((64, 256), F32),
-        pltpu.VMEM((4, 64, 64), F32),
-        pltpu.VMEM((4, 64, 64), F32),
+        pltpu.VMEM((2, 64, 128), F32),
+        pltpu.VMEM((2, 64, 128), F32),
+        pltpu.VMEM((2, 64, 256), F32),
         dma((18,)),
-        dma((2,)), dma((2,)),
+        dma((3,)), dma((3,)),
         dma, dma,
         dma((3,)), dma((4,)),
         dma((2, 2)), dma((2, 2)),
@@ -576,6 +640,7 @@
         dma((2, 2, 2)), dma((2, 2, 2)),
         dma((2, 2)), dma((2, 2)),
         dma, dma, dma, dma,
+        dma, dma,
         pltpu.SemaphoreType.REGULAR,
     ]
     return pl.pallas_call(

time: 42.8 us -> 40.4 us (0.944)
  Pallas kernels: 41.4 us -> 39 us
    pallas_call x1, Pallas kernels: 41.4 us -> 39 us  [per_device(): pl.pallas_call(kernel, out_shape=jax.ShapeDtypeStruct(previous.shape, BF1...]
where the time goes in v4:
time: 40.4 us
  Pallas kernels  39 us (97%)
  local copies, waits for them, and re-layouts  1.32 us (3%)
    pallas_call x1, Pallas kernels, per_device(): pl.pallas_call(kernel, out_shape=jax.ShapeDtypeStruct(previous.shape, BF1...  39 us
    unnamed x1, local copies, waits for them, and re-layouts  1.32 us

profile of v4, /device:TPU:225, one launch (start us, length us, event | category | flops | bytes accessed | tf_op | source)
XLA Modules:
  0.0 40.4 jit_solution(15627626479940898078)
XLA Ops:
  0.0 39.0 %shard_map.82 = bf16[2,1,4,512,256]{4,3,2,1,0:T(8,128)(2,1)S(1)} custom-call(s32[2,1,4]{2,1,0:T(1,128)} %order_in.1, bf16[2,1,4,512,512]{4,3,2,1,0:T(8,128)(2,1)} %inv.1, bf16[2,1,4,64,512]{4,3,2,1,0:T(8,128)(2,1)} %up.1, bf16[2,1,4,64,512]{4,3,2,1,0:T(8,128)(2,1)} %side.1, f32[2,64,256]{2,1,0:T(8,128)} %inlet_in.1, bf16[2,1,4,512,256]{4,3,2,1,0:T(8,128)(2,1)} %prev.1, ...), custom_call_target="tpu_custom_call" | custom-call | tf_op jit(solution)/shard_map/pallas_call | solution.py:646
  39.0 1.3 %copy.10 = bf16[2,1,4,512,256]{4,3,2,1,0:T(8,128)(2,1)} copy(bf16[2,1,4,512,256]{4,3,2,1,0:T(8,128)(2,1)S(1)} %shard_map.82) | data formatting | bytes 4194304

commit v5 on v4

--- a/solution.py
+++ b/solution.py
@@ -53,7 +53,7 @@
     is0 = core == 0
     xs = 4
     bends = (lax.rem(lat, xs) == xs - 1) & (lat < lats - 1)
-    relays = (lax.rem(lat, xs) == 0) & (lat < lats - xs)
+    relays = (lax.rem(lat, xs) == xs - 2) & (lat < lats - 2)
     relayed = (lax.rem(lat, xs) == 0) & (lat > 0)
     partner = {"stream": s + 1 - 2 * core}
 
@@ -81,11 +81,11 @@
 
     @pl.when(relays)
     def _():
-        hello({"lat": lat + xs - 1})
+        hello({"lat": lat + 1})
 
     @pl.when(relayed)
     def _():
-        hello({"lat": lat - xs})
+        hello({"lat": lat - 2})
 
     @pl.when(zhi == 0)
     def _():
@@ -241,18 +241,22 @@
     def s1_copy(it, c):
         return remote(OS.at[it, c, 1 - core], OR.at[it, c], s1_s.at[it, c], s1_r.at[it, c], partner)
 
-    def chain(it, c):
-        for j in range(rows):
-            F[c, j, edge:, :] += apply(NN[c, j, edge:, :], LAT[0, c, j], LAT[1, c, j])
-        h = F[c, order[c, 0, 0], edge:, :]
+    def chain(it, *cs):
+        for c in cs:
+            for j in range(rows):
+                F[c, j, edge:, :] += apply(NN[c, j, edge:, :], LAT[0, c, j], LAT[1, c, j])
+        hs = [F[c, order[c, 0, 0], edge:, :] for c in cs]
         for p in range(1, rows):
-            H[c, p - 1] = h
-            hh, hl = split(h)
-            j = order[c, 0, p]
-            h = F[c, j, edge:, :] + apply(mm_edge(c, j), hh, hl)
-        OS[it, c, 0] = h[:, 0:half]
-        OS[it, c, 1] = h[:, half:]
-        s1_copy(it, c).start()
+            for i, c in enumerate(cs):
+                H[c, p - 1] = hs[i]
+                hh, hl = split(hs[i])
+                j = order[c, 0, p]
+                hs[i] = F[c, j, edge:, :] + apply(mm_edge(c, j), hh, hl)
+        for i, c in enumerate(cs):
+            OS[it, c, 0] = hs[i][:, 0:half]
+            OS[it, c, 1] = hs[i][:, half:]
+        for c in cs:
+            s1_copy(it, c).start()
 
     def first_second(it, c):
         own, got = OS[it, c, core], OR[it, c]
@@ -390,11 +394,11 @@
     back = pl.ds(2, 2)
 
     def bend_copy():
-        peer = {"lat": lax.rem(lat + lats - xs + 1, lats)}
+        peer = {"lat": lax.rem(lat + lats - 1, lats)}
         return remote(LS.at[1, back], RL, lat_s.at[2], rl_r, peer)
 
     def relay_copy():
-        peer = {"lat": lax.rem(lat + xs, lats)}
+        peer = {"lat": lax.rem(lat + 2, lats)}
         return remote(RL, LR.at[1, back], rl_s, lat_r.at[2], peer)
 
     def pass_on():
@@ -512,6 +516,7 @@
     def _():
         enter(0, 1)
 
+    pass_on()
     loads["ar0"].wait()
     maps_rest(0)
     rest(0, early)
@@ -523,15 +528,13 @@
         enter(0, 1)
 
     inflows(0, 1)
-    pass_on()
     lag(1)
     enter(0, 0)
     inflows(0, 0)
     lag(0)
     lat_arrival(1)
 
-    chain(1, 0)
-    chain(1, 1)
+    chain(1, 0, 1)
     compose(1, 0)
     compose(1, 1)
     rest(0, range(rows))

time: 40.4 us -> 39.1 us (0.968)
  Pallas kernels: 39 us -> 37.7 us
    pallas_call x1, Pallas kernels: 39 us -> 37.7 us  [per_device(): pl.pallas_call(kernel, out_shape=jax.ShapeDtypeStruct(previous.shape, BF1...]
where the time goes in v5:
time: 39.1 us
  Pallas kernels  37.7 us (96%)
  local copies, waits for them, and re-layouts  1.32 us (3%)
    pallas_call x1, Pallas kernels, per_device(): pl.pallas_call(kernel, out_shape=jax.ShapeDtypeStruct(previous.shape, BF1...  37.7 us
    unnamed x1, local copies, waits for them, and re-layouts  1.32 us

profile of v5, /device:TPU:225, one launch (start us, length us, event | category | flops | bytes accessed | tf_op | source)
XLA Modules:
  0.0 39.1 jit_solution(7723912206963866341)
XLA Ops:
  0.0 37.7 %shard_map.82 = bf16[2,1,4,512,256]{4,3,2,1,0:T(8,128)(2,1)S(1)} custom-call(s32[2,1,4]{2,1,0:T(1,128)} %order_in.1, bf16[2,1,4,512,512]{4,3,2,1,0:T(8,128)(2,1)} %inv.1, bf16[2,1,4,64,512]{4,3,2,1,0:T(8,128)(2,1)} %up.1, bf16[2,1,4,64,512]{4,3,2,1,0:T(8,128)(2,1)} %side.1, f32[2,64,256]{2,1,0:T(8,128)} %inlet_in.1, bf16[2,1,4,512,256]{4,3,2,1,0:T(8,128)(2,1)} %prev.1, ...), custom_call_target="tpu_custom_call" | custom-call | tf_op jit(solution)/shard_map/pallas_call | solution.py:649
  37.7 1.3 %copy.10 = bf16[2,1,4,512,256]{4,3,2,1,0:T(8,128)(2,1)} copy(bf16[2,1,4,512,256]{4,3,2,1,0:T(8,128)(2,1)S(1)} %shard_map.82) | data formatting | bytes 4194304

commit v6 on v5

--- a/solution.py
+++ b/solution.py
@@ -55,6 +55,7 @@
     bends = (lax.rem(lat, xs) == xs - 1) & (lat < lats - 1)
     relays = (lax.rem(lat, xs) == xs - 2) & (lat < lats - 2)
     relayed = (lax.rem(lat, xs) == 0) & (lat > 0)
+    starts = (lax.rem(lat, xs) == 0) & (lat < lats - xs)
     partner = {"stream": s + 1 - 2 * core}
 
     def ypeer(d):
@@ -83,9 +84,14 @@
     def _():
         hello({"lat": lat + 1})
 
+    @pl.when(starts)
+    def _():
+        hello({"lat": lat + xs - 1})
+
     @pl.when(relayed)
     def _():
         hello({"lat": lat - 2})
+        hello({"lat": lat - xs})
 
     @pl.when(zhi == 0)
     def _():
@@ -93,7 +99,7 @@
         hello(above(1))
 
     expected = 4 + jnp.where(lat < lats - 1, 1, 0) + jnp.where(zhi == 1, 2, 0)
-    expected = expected + jnp.where(bends, 1, 0) + jnp.where(relays, 1, 0)
+    expected = expected + jnp.where(bends, 2, 0) + jnp.where(relays | starts, 1, 0)
 
     loads = {}
 
@@ -376,11 +382,13 @@
         @pl.when((lat < lats - 1) & jnp.logical_not(bends))
         def _():
             part_copy(1).start()
+            part_copy(2).start()
             r_copy().start()
 
         @pl.when(bends)
         def _():
-            bend_copy().start()
+            bend_copy(0).start()
+            bend_copy(1).start()
 
     def map_send():
         @pl.when(bends)
@@ -388,24 +396,22 @@
             r_copy().start()
 
     def part_copy(k):
-        js = pl.ds(2 * k, 2)
+        js = pl.ds(0, 2) if k == 0 else pl.ds(1 + k, 1)
         return remote(LS.at[1, js], LR.at[1, js], lat_s.at[1 + k], lat_r.at[1 + k], {"lat": lax.rem(lat + 1, lats)})
 
-    back = pl.ds(2, 2)
-
-    def bend_copy():
-        peer = {"lat": lax.rem(lat + lats - 1, lats)}
-        return remote(LS.at[1, back], RL, lat_s.at[2], rl_r, peer)
-
-    def relay_copy():
-        peer = {"lat": lax.rem(lat + 2, lats)}
-        return remote(RL, LR.at[1, back], rl_s, lat_r.at[2], peer)
-
-    def pass_on():
-        @pl.when(relays)
-        def _():
-            bend_copy().wait_recv()
-            relay_copy().start()
+    def bend_copy(k):
+        peer = {"lat": lax.rem(lat + lats - (xs - 1 if k else 1), lats)}
+        return remote(LS.at[1, pl.ds(2 + k, 1)], RL, lat_s.at[2 + k], rl_r, peer)
+
+    def relay_copy(k):
+        peer = {"lat": lax.rem(lat + (xs if k else 2), lats)}
+        return remote(RL, LR.at[1, pl.ds(2 + k, 1)], rl_s, lat_r.at[2 + k], peer)
+
+    def pass_on(k):
+        @pl.when(starts if k else relays)
+        def _():
+            bend_copy(k).wait_recv()
+            relay_copy(k).start()
 
     def lag(c):
         for j in range(rows):
@@ -426,7 +432,7 @@
             if it == 0:
                 lat_copy(it).wait_recv()
             else:
-                for k in range(2):
+                for k in range(3):
                     part_copy(k).wait_recv()
                 r_copy().wait_recv()
                 x_copy().wait_recv()
@@ -516,11 +522,12 @@
     def _():
         enter(0, 1)
 
-    pass_on()
+    pass_on(0)
     loads["ar0"].wait()
     maps_rest(0)
     rest(0, early)
     gather(0, 0)
+    pass_on(1)
     rest(0, late)
 
     @pl.when(zhi == 1)
@@ -558,14 +565,16 @@
             if it == 0:
                 lat_copy(it).wait_send()
             else:
-                for k in range(2):
+                for k in range(3):
                     part_copy(k).wait_send()
 
         if it == 1:
 
-            @pl.when(relays)
-            def _():
-                relay_copy().wait_send()
+            for k in range(2):
+
+                @pl.when(starts if k else relays)
+                def _():
+                    relay_copy(k).wait_send()
 
     t_copy.wait_send()
     for d in range(1, YS):
@@ -633,9 +642,9 @@
         pltpu.VMEM((64, 256), F32),
         pltpu.VMEM((2, 64, 128), F32),
         pltpu.VMEM((2, 64, 128), F32),
-        pltpu.VMEM((2, 64, 256), F32),
+        pltpu.VMEM((1, 64, 256), F32),
         dma((18,)),
-        dma((3,)), dma((3,)),
+        dma((4,)), dma((4,)),
         dma, dma,
         dma((3,)), dma((4,)),
         dma((2, 2)), dma((2, 2)),

time: 39.1 us -> 38.4 us (0.982)
  Pallas kernels: 37.7 us -> 37 us
    pallas_call x1, Pallas kernels: 37.7 us -> 37 us  [per_device(): pl.pallas_call(kernel, out_shape=jax.ShapeDtypeStruct(previous.shape, BF1...]
where the time goes in v6:
time: 38.4 us; the launch traced here: 38.3 us
  Pallas kernels  37 us (96%)
  local copies, waits for them, and re-layouts  1.32 us (3%)
    pallas_call x1, Pallas kernels, per_device(): pl.pallas_call(kernel, out_shape=jax.ShapeDtypeStruct(previous.shape, BF1...  37 us
    unnamed x1, local copies, waits for them, and re-layouts  1.32 us

profile of v6, /device:TPU:225, one launch (start us, length us, event | category | flops | bytes accessed | tf_op | source)
XLA Modules:
  0.0 38.3 jit_solution(11214521645135234152)
XLA Ops:
  0.0 37.0 %shard_map.82 = bf16[2,1,4,512,256]{4,3,2,1,0:T(8,128)(2,1)S(1)} custom-call(s32[2,1,4]{2,1,0:T(1,128)} %order_in.1, bf16[2,1,4,512,512]{4,3,2,1,0:T(8,128)(2,1)} %inv.1, bf16[2,1,4,64,512]{4,3,2,1,0:T(8,128)(2,1)} %up.1, bf16[2,1,4,64,512]{4,3,2,1,0:T(8,128)(2,1)} %side.1, f32[2,64,256]{2,1,0:T(8,128)} %inlet_in.1, bf16[2,1,4,512,256]{4,3,2,1,0:T(8,128)(2,1)} %prev.1, ...), custom_call_target="tpu_custom_call" | custom-call | tf_op jit(solution)/shard_map/pallas_call | solution.py:658
  37.0 1.3 %copy.10 = bf16[2,1,4,512,256]{4,3,2,1,0:T(8,128)(2,1)} copy(bf16[2,1,4,512,256]{4,3,2,1,0:T(8,128)(2,1)S(1)} %shard_map.82) | data formatting | bytes 4194304
